TPU v7x, 256 devices: a whole 4x4x8 slice. The times are simulated.
256 devices in a mesh: row: 16 (over x_lo, z), col: 16 (over x_hi, y, core).
Axes of the slice: x: 4 (x_hi: 2, x_lo: 2; x = x_hi * 2 + x_lo), y: 4, z: 8, core: 2. Of those that a mesh axis runs over, the one named last changes fastest.
Arguments:
- cov: float32 [16384, 16384], P('row', 'col'), as said below
- noise: float32 [16384, 16384], P('row', 'col'), as said below
- diffusivity: float32 [128, 128], P('row'), may hold values from 0.25 to 1
- wind_x: float32 [128, 128], P('row'), may hold values from -1 to 1
- wind_y: float32 [128, 128], P('row'), may hold values from -1 to 1
Outputs:
- cov_next: float32 [16384, 16384], P('row', 'col')
Inputs may be any that keep to these rules, and one draw needn't show every extreme that they name: cov is symmetric. noise is symmetric.
All inputs are finite; a program needn't handle non-finite values.
Results may differ from a plain program's by a relative error of at most 0.00002.
Values sent between devices are 32-bit elements; how exact they have to be, the bound alone decides.
No kernel may reach another device: no remote copies, remote signals or barrier semaphores. Data moves between devices by JAX's collectives and lax.ppermute only.
A program may use at most 192 MiB of HBM per device.

v0:
```python
import jax
import jax.numpy as jnp
from jax import lax
from jax.sharding import PartitionSpec as P

OFFSETS = ((0, 0), (1, 0), (-1, 0), (0, 1), (0, -1), (1, 1), (1, -1), (-1, 1), (-1, -1))
time_step = 0.1


def sent_together(arrays, axis, dim, along):
    ends, at = ([], 0)
    for a in arrays[:-1]:
        at += a.shape[along]
        ends.append(at)
    both = jnp.concatenate(arrays, axis=along)
    return tuple(jnp.split(lax.all_gather(both, axis, axis=dim, tiled=True), ends, axis=along))


def extended(value, sides, width):
    edges = {}
    for axis, dim in sides:
        count, length = (lax.axis_size(axis), value.shape[dim])
        up = [(i, (i + 1) % count) for i in range(count - 1)]
        last = lax.slice_in_dim(value, length - width, length, axis=dim)
        leading = lax.slice_in_dim(value, 0, width, axis=dim)
        edges[dim] = (
            lax.ppermute(last, axis, up),
            lax.ppermute(leading, axis, [(b, a) for a, b in up]),
        )
    done = []
    for _, dim in sides:
        low, high = edges[dim]
        around = [(width, width) if d in done else (0, 0) for d in range(value.ndim)]
        value = jnp.concatenate([jnp.pad(low, around), value, jnp.pad(high, around)], axis=dim)
        done.append(dim)
    return value


def stencil_weights(kappa, flow_x, flow_y):
    edge = 4.0 / 6.0 * kappa
    corner = kappa / 6.0
    return jnp.stack(
        [
            -20.0 / 6.0 * kappa,
            edge - 0.5 * flow_x,
            edge + 0.5 * flow_x,
            edge - 0.5 * flow_y,
            edge + 0.5 * flow_y,
            corner,
            corner,
            corner,
            corner,
        ]
    )


def row_term(padded, weights):
    count = weights.shape[1]
    side = weights.shape[2]
    wide = jnp.pad(padded, ((0, 0), (1, 1), (0, 0)))
    total = jnp.zeros((count, side, padded.shape[2]), jnp.float32)
    for index, (step_x, step_y) in enumerate(OFFSETS):
        piece = wide[1 + step_x : 1 + step_x + count, 1 + step_y : 1 + step_y + side, :]
        total = total + weights[index][:, :, None] * piece
    return total


def col_term(padded, weights):
    count = weights.shape[1]
    side = weights.shape[2]
    wide = jnp.pad(padded, ((0, 0), (0, 0), (1, 1)))
    total = jnp.zeros((padded.shape[0], count, side), jnp.float32)
    for index, (step_x, step_y) in enumerate(OFFSETS):
        piece = wide[:, 1 + step_x : 1 + step_x + count, 1 + step_y : 1 + step_y + side]
        total = total + weights[index][None, :, :] * piece
    return total


def derive(padded, noise, row_weights, col_weights, side):
    rows = padded.shape[0] - 2 * side
    cols = padded.shape[1] - 2 * side
    middle_cols = padded[:, side : side + cols].reshape(rows // side + 2, side, cols)
    middle_rows = padded[side : side + rows, :].reshape(rows, cols // side + 2, side)
    along_rows = row_term(middle_cols, row_weights).reshape(rows, cols)
    along_cols = col_term(middle_rows, col_weights).reshape(rows, cols)
    return along_rows + along_cols + noise


def per_device(cov, noise, diffusivity, wind_x, wind_y):
    kappa, flow_x, flow_y = sent_together((diffusivity, wind_x, wind_y), "row", 0, 1)
    weights = stencil_weights(kappa, flow_x, flow_y)
    side = weights.shape[2]
    framed = jnp.pad(weights, ((0, 0), (1, 1), (0, 0)))
    row_count = cov.shape[0] // side
    col_count = cov.shape[1] // side
    row_start = lax.axis_index("row") * row_count
    col_start = lax.axis_index("col") * col_count
    row_wide = lax.dynamic_slice_in_dim(framed, row_start, row_count + 2, 1)
    col_wide = lax.dynamic_slice_in_dim(framed, col_start, col_count + 2, 1)
    row_inner = row_wide[:, 1:-1]
    col_inner = col_wide[:, 1:-1]

    def advance(field):
        padded = extended(field, (("row", 0), ("col", 1)), side)
        return derive(padded, noise, row_inner, col_inner, side)

    first = advance(cov)
    middle = cov + time_step * first
    second = advance(middle)
    return cov + 0.5 * time_step * (first + second)


def solution(mesh):
    return jax.shard_map(
        per_device,
        mesh=mesh,
        in_specs=(P("row", "col"), P("row", "col"), P("row", None), P("row", None), P("row", None)),
        out_specs=P("row", "col"),
        check_vma=False,
    )
```

profile of v0, /device:TPU:25, one launch (start us, length us, event | category | flops | bytes accessed | tf_op | source)
XLA Modules:
  0.0 210.4 jit_solution(86815715610824306)
XLA Ops:
  0.0 0.0 copy-start.6
  0.0 2.3 %fusion.81 = (f32[128,1024]{1,0:T(8,128)}, f32[128,1024]{1,0:T(8,128)}) fusion(f32[1024,1024]{1,0:T(8,128)} %param.5), kind=kLoop, calls=%fused_computation.163 | loop fusion | bytes 2097152 | tf_op jit(solution)/shard_map/slice | solution.py:25
  2.3 3.6 %collective-permute-start.1 = (f32[128,1024]{1,0:T(8,128)}, f32[128,1024]{1,0:T(8,128)S(1)}, u32[]{:S(2)}, u32[]{:S(2)}) collective-permute-start(f32[128,1024]{1,0:T(8,128)} %get-tuple-element.17), channel_id=1, source_target_pairs={{0,16},{16,32},{32,48},{48,64},{64,80},{80,96},{96,112},{112,128},... | collective-permute-start | bytes 1572872 | tf_op jit(solution)/shard_map/ppermute | solution.py:27
  5.9 1.3 collective-permute-start
  7.2 2.1 fusion.80
  9.3 5.1 %collective-permute-start.2 = (f32[1024,128]{1,0:T(8,128)}, f32[1024,128]{1,0:T(8,128)S(1)}, u32[]{:S(2)}, u32[]{:S(2)}) collective-permute-start(f32[1024,128]{1,0:T(8,128)} %get-tuple-element.14), channel_id=1, source_target_pairs={{0,1},{1,2},{2,3},{3,4},{4,5},{5,6},{6,7},{7,8},{8,9},{9,10},{10,1... | collective-permute-start | bytes 1572872 | tf_op jit(solution)/shard_map/ppermute | solution.py:27
  14.4 1.9 collective-permute-start.3
  16.4 0.0 copy-done.6
  16.4 0.0 copy-done.5
  16.4 0.0 copy-done.4
  16.4 30.0 %all_gather.3 = f32[128,384]{1,0:T(8,128)S(1)} all-gather(f32[8,384]{1,0:T(8,128)S(1)} %pad_maximum_fusion.8), channel_id=1, replica_groups=mesh['row'=16,'col'=16] {'row'}, dimensions={0}, use_global_device_ids=true | all-gather | bytes 208896 | tf_op jit(solution)/shard_map/all_gather | solution.py:16
  46.7 0.1 fusion.60
  46.7 0.0 collective-permute-done.1
  46.7 0.8 constant_dynamic-update-slice_fusion.2
  47.6 0.0 collective-permute-done
  47.6 10.0 %pad_maximum_fusion.7 = (f32[1024,1024]{1,0:T(8,128)}, f32[1280,1024]{1,0:T(8,128)}, f32[1024,1024]{1,0:T(8,128)}) fusion(f32[128,1024]{1,0:T(8,128)S(1)} %collective-permute-done, f32[1024,1024]{1,0:T(8,128)} %param.5, f32[1280,1024]{1,0:T(8,128)} %constant_dynamic-update-slice_fusion.2, f32[128,1024]{1,0:T(8,128)S(1)} %collective-permute-done.1), kind=kLoop, calls=%fused_computation.98 | loop fusion | flops 2097152 | bytes 17825792 | tf_op jit(solution)/shard_map/concatenate | solution.py:34
  57.6 0.8 constant_dynamic-update-slice_fusion
  58.4 0.0 collective-permute-done.2
  58.4 0.0 collective-permute-done.3
  58.4 4.9 %fusion.2 = f32[1024,1280]{1,0:T(8,128)} fusion(f32[1024,128]{1,0:T(8,128)S(1)} %collective-permute-done.3, f32[1280,1024]{1,0:T(8,128)} %constant_dynamic-update-slice_fusion, f32[1024,128]{1,0:T(8,128)S(1)} %collective-permute-done.2), kind=kLoop, calls=%fused_computation.7 | loop fusion | flops 7864320 | bytes 11534336 | tf_op jit(solution)/shard_map/concatenate | solution.py:34
  63.3 6.0 %copy.21 = f32[1024,1280]{0,1:T(8,128)} copy(f32[1024,1280]{1,0:T(8,128)} %fusion.2) | data formatting | bytes 10485760 | tf_op jit(solution)/shard_map/slice | solution.py:83
  69.2 19.5 %fusion.21 = f32[1024,8,128]{0,2,1:T(8,128)} fusion(f32[1024,10,128]{0,2,1:T(8,128)} %bitcast.83, f32[8,128]{1,0:T(8,128)S(1)} %get-tuple-element.19, f32[8,128]{1,0:T(8,128)S(1)} %get-tuple-element.29, f32[8,128]{1,0:T(8,128)S(1)} %get-tuple-element.26, f32[8,128]{1,0:T(8,128)S(1)} %get-tuple-element.25, f32[8,128]{1,0:T(8,128)S(1)} %get-tuple-element.24, ...), kind=kLoop, calls=%fused_computation.55 | loop fusion | flops 17825792 | bytes 22056960 | tf_op jit(solution)/shard_map/add | solution.py:75
  88.7 5.4 %copy.22 = f32[1024,1024]{1,0:T(8,128)} copy(f32[1024,1024]{0,1:T(8,128)} %bitcast.92) | data formatting | bytes 8388608 | tf_op jit(solution)/shard_map/reshape | solution.py:85
  94.2 17.7 %fusion.9 = f32[8,128,1024]{2,1,0:T(8,128)} fusion(f32[10,128,1024]{2,1,0:T(8,128)} %bitcast.85, f32[8,128,1024]{2,1,0:T(8,128)} %bitcast.88, f32[8,128,1024]{2,1,0:T(8,128)} %bitcast.87, f32[8,128,1024]{2,1,0:T(8,128)} %bitcast.84, f32[8,128]{1,0:T(8,128)S(1)} %get-tuple-element.27, f32[8,128]{1,0:T(8,128)S(1)} %get-tuple-element.30, ...), kind=kLoop, calls=%fused_computation.43 | loop fusion | flops 17825792 | bytes 22056960 | tf_op jit(solution)/shard_map/add | solution.py:64
  111.9 0.0 copy-done.2
  111.9 0.0 copy-done.3
  111.9 5.5 %multiply_add_fusion = f32[1024,1024]{1,0:T(8,128)S(1)} fusion(f32[1024,1024]{1,0:T(8,128)S(1)} %copy-done.2, f32[1024,1024]{1,0:T(8,128)} %param.6, f32[1024,1024]{1,0:T(8,128)S(1)} %copy-done.3, f32[8,128,1024]{2,1,0:T(8,128)} %fusion.9), kind=kLoop, calls=%fused_computation.106 | loop fusion | flops 4194304 | bytes 20971520 | tf_op jit(solution)/shard_map/add | solution.py:108
  117.4 0.0 copy-start
  117.4 0.1 fusion.78
  117.5 0.1 fusion.79
  117.6 1.3 collective-permute-start.4
  118.9 4.0 %collective-permute-start.5 = (f32[128,1024]{1,0:T(8,128)S(1)}, f32[128,1024]{1,0:T(8,128)S(1)}, u32[]{:S(2)}, u32[]{:S(2)}) collective-permute-start(f32[128,1024]{1,0:T(8,128)S(1)} %get-tuple-element.7), channel_id=1, source_target_pairs={{0,16},{16,32},{32,48},{48,64},{64,80},{80,96},{96,112},{112,128},... | collective-permute-start | bytes 1572872 | tf_op jit(solution)/shard_map/ppermute | solution.py:27
  122.9 15.7 %collective-permute-start.6 = (f32[1024,128]{1,0:T(8,128)S(1)}, f32[1024,128]{1,0:T(8,128)S(1)}, u32[]{:S(2)}, u32[]{:S(2)}) collective-permute-start(f32[1024,128]{1,0:T(8,128)S(1)} %get-tuple-element.9), channel_id=1, source_target_pairs={{0,1},{1,2},{2,3},{3,4},{4,5},{5,6},{6,7},{7,8},{8,9},{9,10},{10,1... | collective-permute-start | bytes 1572872 | tf_op jit(solution)/shard_map/ppermute | solution.py:27
  138.6 2.1 collective-permute-start.7
  140.7 0.0 collective-permute-done.4
  140.7 0.0 collective-permute-done.5
  140.7 4.0 %collective-permute-done.6 = f32[1024,128]{1,0:T(8,128)S(1)} collective-permute-done((f32[1024,128]{1,0:T(8,128)S(1)}, f32[1024,128]{1,0:T(8,128)S(1)}, u32[]{:S(2)}, u32[]{:S(2)}) %collective-permute-start.6) | collective-permute-done | bytes 524320 | tf_op jit(solution)/shard_map/ppermute | solution.py:27
  144.7 8.0 %collective-permute-done.7 = f32[1024,128]{1,0:T(8,128)S(1)} collective-permute-done((f32[1024,128]{1,0:T(8,128)S(1)}, f32[1024,128]{1,0:T(8,128)S(1)}, u32[]{:S(2)}, u32[]{:S(2)}) %collective-permute-start.7) | collective-permute-done | bytes 524320 | tf_op jit(solution)/shard_map/ppermute | solution.py:28
  152.7 0.0 copy-done
  152.7 2.6 %fusion = f32[1024,1280]{1,0:T(8,128)} fusion(f32[1024,128]{1,0:T(8,128)S(1)} %collective-permute-done.7, f32[1024,128]{1,0:T(8,128)S(1)} %collective-permute-done.6, f32[128,1024]{1,0:T(8,128)S(1)} %collective-permute-done.4, f32[1024,1024]{1,0:T(8,128)S(1)} %multiply_add_fusion, f32[128,1024]{1,0:T(8,128)S(1)} %collective-permute-done.5), kind=kLoop, calls=%fused_computation.1 | loop fusion | flops 10485760 | bytes 11534336 | tf_op jit(solution)/shard_map/concatenate | solution.py:34
  155.3 5.9 %copy.23 = f32[1024,1280]{0,1:T(8,128)} copy(f32[1024,1280]{1,0:T(8,128)} %fusion) | data formatting | bytes 10485760 | tf_op jit(solution)/shard_map/slice | solution.py:83
  161.2 19.3 %fusion.45 = f32[1024,8,128]{0,2,1:T(8,128)} fusion(f32[1024,10,128]{0,2,1:T(8,128)} %bitcast.82, f32[8,128]{1,0:T(8,128)S(1)} %get-tuple-element.19, f32[8,128]{1,0:T(8,128)S(1)} %get-tuple-element.29, f32[8,128]{1,0:T(8,128)S(1)} %get-tuple-element.26, f32[8,128]{1,0:T(8,128)S(1)} %get-tuple-element.25, f32[8,128]{1,0:T(8,128)S(1)} %get-tuple-element.24, ...), kind=kLoop, calls=%fused_computation.79 | loop fusion | flops 17825792 | bytes 22056960 | tf_op jit(solution)/shard_map/add | solution.py:75
  180.6 5.4 %copy.24 = f32[1024,1024]{1,0:T(8,128)} copy(f32[1024,1024]{0,1:T(8,128)} %bitcast.91) | data formatting | bytes 8388608 | tf_op jit(solution)/shard_map/reshape | solution.py:85
  186.0 4.2 %pad_maximum_fusion.5 = (f32[1024,1024]{1,0:T(8,128)S(1)}, f32[1024,1024]{1,0:T(8,128)S(1)}) fusion(f32[128,1024]{1,0:T(8,128)S(1)} %collective-permute-done.4, f32[1024,1024]{1,0:T(8,128)} %copy-done, f32[128,1024]{1,0:T(8,128)S(1)} %collective-permute-done.5), kind=kLoop, calls=%fused_computation.91 | loop fusion | flops 2097152 | bytes 13631488 | tf_op jit(solution)/shard_map/concatenate | solution.py:34
  190.2 0.1 copy-done.1
  190.3 0.8 pad_maximum_fusion.3
  191.2 5.4 %fusion.33 = f32[8,128,1024]{2,1,0:T(8,128)} fusion(f32[10,128,1024]{2,1,0:T(8,128)S(1)} %bitcast.86, f32[8,128,1024]{2,1,0:T(8,128)S(1)} %bitcast.90, f32[8,128,1024]{2,1,0:T(8,128)S(1)} %bitcast.89, f32[8,128,1024]{2,1,0:T(8,128)S(1)} %bitcast.81, f32[8,128]{1,0:T(8,128)S(1)} %get-tuple-element.27, f32[8,128]{1,0:T(8,128)S(1)} %get-tuple-element.30, ...), kind=kLoop, calls=%fused_computation.67 | loop fusion | flops 17825792 | bytes 22056960 | tf_op jit(solution)/shard_map/add | solution.py:64
  196.5 13.9 %fusion.58 = f32[1024,1024]{1,0:T(8,128)} fusion(f32[1024,1024]{1,0:T(8,128)} %param.5, f32[1024,1024]{1,0:T(8,128)} %param.6, f32[1024,1024]{1,0:T(8,128)} %copy.24, f32[8,128,1024]{2,1,0:T(8,128)} %fusion.33, f32[1024,1024]{1,0:T(8,128)} %copy.22, f32[8,128,1024]{2,1,0:T(8,128)} %fusion.9), kind=kLoop, calls=%fused_computation.103 | loop fusion | flops 7340032 | bytes 29360128 | tf_op jit(solution)/shard_map/add | solution.py:110
  (16 shorter events, 0.2 us)
Async XLA Ops:
  0.0 16.4 %copy-start.6 = (f32[8,128]{1,0:T(8,128)S(1)}, f32[8,128]{1,0:T(8,128)}, u32[]{:S(2)}) copy-start(f32[8,128]{1,0:T(8,128)} %param.7) | copy-start | bytes 12292
  0.0 16.4 %copy-start.5 = (f32[8,128]{1,0:T(8,128)S(1)}, f32[8,128]{1,0:T(8,128)}, u32[]{:S(2)}) copy-start(f32[8,128]{1,0:T(8,128)} %param.8) | copy-start | bytes 12292
  0.0 16.4 %copy-start.4 = (f32[8,128]{1,0:T(8,128)S(1)}, f32[8,128]{1,0:T(8,128)}, u32[]{:S(2)}) copy-start(f32[8,128]{1,0:T(8,128)} %param.9) | copy-start | bytes 12292
  2.3 44.4 %collective-permute-start.1 = (f32[128,1024]{1,0:T(8,128)}, f32[128,1024]{1,0:T(8,128)S(1)}, u32[]{:S(2)}, u32[]{:S(2)}) collective-permute-start(f32[128,1024]{1,0:T(8,128)} %get-tuple-element.17), channel_id=1, source_target_pairs={{0,16},{16,32},{32,48},{48,64},{64,80},{80,96},{96,112},{112,128},... | collective-permute-start | bytes 1572872 | tf_op jit(solution)/shard_map/ppermute | solution.py:27
  5.9 41.7 %collective-permute-start = (f32[128,1024]{1,0:T(8,128)}, f32[128,1024]{1,0:T(8,128)S(1)}, u32[]{:S(2)}, u32[]{:S(2)}) collective-permute-start(f32[128,1024]{1,0:T(8,128)} %get-tuple-element.16), channel_id=1, source_target_pairs={{16,0},{32,16},{48,32},{64,48},{80,64},{96,80},{112,96},{128,112},... | collective-permute-start | bytes 1572872 | tf_op jit(solution)/shard_map/ppermute | solution.py:28
  9.3 49.1 %collective-permute-start.2 = (f32[1024,128]{1,0:T(8,128)}, f32[1024,128]{1,0:T(8,128)S(1)}, u32[]{:S(2)}, u32[]{:S(2)}) collective-permute-start(f32[1024,128]{1,0:T(8,128)} %get-tuple-element.14), channel_id=1, source_target_pairs={{0,1},{1,2},{2,3},{3,4},{4,5},{5,6},{6,7},{7,8},{8,9},{9,10},{10,1... | collective-permute-start | bytes 1572872 | tf_op jit(solution)/shard_map/ppermute | solution.py:27
  14.4 44.0 %collective-permute-start.3 = (f32[1024,128]{1,0:T(8,128)S(1)}, f32[1024,128]{1,0:T(8,128)S(1)}, u32[]{:S(2)}, u32[]{:S(2)}) collective-permute-start(f32[1024,128]{1,0:T(8,128)S(1)} %get-tuple-element.15), channel_id=1, source_target_pairs={{1,0},{2,1},{3,2},{4,3},{5,4},{6,5},{7,6},{8,7},{9,8},{10,9},{11,1... | collective-permute-start | bytes 1572872 | tf_op jit(solution)/shard_map/ppermute | solution.py:28
  94.1 17.7 %copy-start.2 = (f32[1024,1024]{1,0:T(8,128)S(1)}, f32[1024,1024]{1,0:T(8,128)}, u32[]{:S(2)}) copy-start(f32[1024,1024]{1,0:T(8,128)} %param.5) | copy-start | bytes 12582916
  94.1 17.7 %copy-start.3 = (f32[1024,1024]{1,0:T(8,128)S(1)}, f32[1024,1024]{1,0:T(8,128)}, u32[]{:S(2)}) copy-start(f32[1024,1024]{1,0:T(8,128)} %copy.22) | copy-start | bytes 12582916
  117.4 35.3 %copy-start = (f32[1024,1024]{1,0:T(8,128)}, f32[1024,1024]{1,0:T(8,128)S(1)}, u32[]{:S(2)}) copy-start(f32[1024,1024]{1,0:T(8,128)S(1)} %multiply_add_fusion) | copy-start | bytes 12582916
  117.6 23.1 %collective-permute-start.4 = (f32[128,1024]{1,0:T(8,128)S(1)}, f32[128,1024]{1,0:T(8,128)S(1)}, u32[]{:S(2)}, u32[]{:S(2)}) collective-permute-start(f32[128,1024]{1,0:T(8,128)S(1)} %get-tuple-element.8), channel_id=1, source_target_pairs={{16,0},{32,16},{48,32},{64,48},{80,64},{96,80},{112,96},{128,112},... | collective-permute-start | bytes 1572872 | tf_op jit(solution)/shard_map/ppermute | solution.py:28
  118.9 21.8 %collective-permute-start.5 = (f32[128,1024]{1,0:T(8,128)S(1)}, f32[128,1024]{1,0:T(8,128)S(1)}, u32[]{:S(2)}, u32[]{:S(2)}) collective-permute-start(f32[128,1024]{1,0:T(8,128)S(1)} %get-tuple-element.7), channel_id=1, source_target_pairs={{0,16},{16,32},{32,48},{48,64},{64,80},{80,96},{96,112},{112,128},... | collective-permute-start | bytes 1572872 | tf_op jit(solution)/shard_map/ppermute | solution.py:27
  122.9 21.8 %collective-permute-start.6 = (f32[1024,128]{1,0:T(8,128)S(1)}, f32[1024,128]{1,0:T(8,128)S(1)}, u32[]{:S(2)}, u32[]{:S(2)}) collective-permute-start(f32[1024,128]{1,0:T(8,128)S(1)} %get-tuple-element.9), channel_id=1, source_target_pairs={{0,1},{1,2},{2,3},{3,4},{4,5},{5,6},{6,7},{7,8},{8,9},{9,10},{10,1... | collective-permute-start | bytes 1572872 | tf_op jit(solution)/shard_map/ppermute | solution.py:27
  138.6 14.1 %collective-permute-start.7 = (f32[1024,128]{1,0:T(8,128)S(1)}, f32[1024,128]{1,0:T(8,128)S(1)}, u32[]{:S(2)}, u32[]{:S(2)}) collective-permute-start(f32[1024,128]{1,0:T(8,128)S(1)} %get-tuple-element.10), channel_id=1, source_target_pairs={{1,0},{2,1},{3,2},{4,3},{5,4},{6,5},{7,6},{8,7},{9,8},{10,9},{11,1... | collective-permute-start | bytes 1572872 | tf_op jit(solution)/shard_map/ppermute | solution.py:28
  186.0 4.3 %copy-start.1 = (f32[1024,1024]{1,0:T(8,128)S(1)}, f32[1024,1024]{1,0:T(8,128)}, u32[]{:S(2)}) copy-start(f32[1024,1024]{1,0:T(8,128)} %copy-done) | copy-start | bytes 12582916
where the time goes:
time: 211 us; the launch traced here: 210 us
  other arithmetic  104 us (49%)
  starting transfers between devices  35 us (17%)
  blocking collectives  30 us (14%)
  local copies, waits for them, and re-layouts  29.2 us (14%)
  waiting for transfers between devices  12 us (6%)
    add x2, other arithmetic, col_term(): total = total + weights[index][None, :, :] * piece  38.8 us
    all_gather x1, blocking collectives, sent_together(): lax.all_gather(both, axis, axis=dim, tiled=True)  30 us
    ppermute x4, starting transfers between devices, extended(): lax.ppermute(last, axis, up)  28.4 us
    add x2, other arithmetic, row_term(): total = total + weights[index][:, :, None] * piece  23.1 us
    concatenate x5, other arithmetic, extended(): jnp.concatenate([jnp.pad(low, around), value, jnp.pad(high, around)], axi...  22.5 us
    add x1, other arithmetic, per_device(): return cov + 0.5 * time_step * (first + second)  13.9 us
    slice x2, local copies, waits for them, and re-layouts, derive(): padded[side:side + rows, :].reshape(rows, cols // side + 2, side)  11.9 us
    reshape x2, local copies, waits for them, and re-layouts, derive(): along_cols = col_term(middle_rows, col_weights).reshape(rows, cols)  10.8 us
  transfers between devices with their start and end apart: 8, of which 2 were waited for; matrix products, arithmetic and copies ran while one was open for 7% of the time, Pallas kernels for 0%

commit v1 on v0

v1 whole, which is shorter than its diff:
```python
import functools

import jax
import jax.numpy as jnp
from jax import lax
from jax.experimental import pallas as pl
from jax.experimental.pallas import tpu as pltpu
from jax.sharding import PartitionSpec as P

T = 128
LANES = 128
F32 = jnp.float32
STEP = 0.1
SECOND = 0.5 * STEP * STEP


def seven(kappa, flow_x, flow_y):
    edge = (4.0 / 6.0) * kappa
    corner = kappa / 6.0
    at = lax.broadcasted_iota(jnp.int32, kappa.shape, 1)

    def from_above(v):
        return jnp.where(at == 0, 0.0, pltpu.roll(v, 1, 1))

    def from_below(v):
        return jnp.where(at == T - 1, 0.0, pltpu.roll(v, T - 1, 1))

    return [
        (-20.0 / 6.0) * kappa,
        edge - 0.5 * flow_x,
        edge + 0.5 * flow_x,
        from_above(edge - 0.5 * flow_y),
        from_above(corner),
        from_below(edge + 0.5 * flow_y),
        from_below(corner),
    ]


def columns(lists):
    rows = list(lists)
    have = 8 * len(rows)
    if have < LANES:
        rows.append(jnp.zeros((LANES - have, LANES), F32))
    return jnp.concatenate(rows, axis=0).T


def spread(cols, j, x):
    return jnp.broadcast_to(cols[:, 8 * j + x : 8 * j + x + 1], (T, LANES))


def shifted(up, down, axis):
    return pltpu.roll(up, T - 1, axis) + pltpu.roll(down, 1, axis)


def full(mid, low, high, w, axis):
    both = low + high
    return w[0] * mid + w[1] * high + w[2] * low + shifted(w[3] * mid + w[4] * both, w[5] * mid + w[6] * both, axis)


def off(value, w, side, axis):
    return w[side] * value + shifted(w[4] * value, w[6] * value, axis)


def own(value, w, axis):
    return w[0] * value + shifted(w[3] * value, w[5] * value, axis)


def tile(i):
    return slice(i * T, (i + 1) * T)


def at_tile(i):
    return pl.ds(pl.multiple_of(i * T, T), T)


def cp(**kw):
    return pltpu.CompilerParams(vmem_limit_bytes=48 << 20, **kw)


def vmem():
    return pl.BlockSpec(memory_space=pltpu.VMEM)


def hbm():
    return pl.BlockSpec(memory_space=pl.ANY)


def row_edges_body(pt, pb, qt, qb, k, u, w, top, bottom, wide):
    x_last = 7

    @pl.when(pl.program_id(0) == 0)
    def _():
        cols = columns(seven(k[...], u[...], w[...]))
        for j in range(7):
            wide[0, j] = spread(cols, j, 0)
            wide[1, j] = spread(cols, j, x_last)

    for h in range(pt.shape[1] // T):
        lanes = tile(h)
        for m, n, q, out, i, side in (
            (pt[0:T, lanes], pt[T : 2 * T, lanes], qt[:, lanes], top, 0, 1),
            (pb[T : 2 * T, lanes], pb[0:T, lanes], qb[:, lanes], bottom, 1, 2),
        ):
            e = [wide[i, j] for j in range(7)]
            out[0:T, lanes] = q + own(m, e, 0) + off(n, e, side, 0)
            out[T : T + 8, lanes] = jnp.zeros((8, T), F32)

    @pl.when(pl.program_id(0) == 0)
    def _():
        for out, x in ((top, 0), (bottom, x_last)):
            out[T : T + 1, 0:T] = k[x : x + 1, :]
            out[T : T + 1, T : 2 * T] = u[x : x + 1, :]


def row_edges(cov, noise, k, u, w):
    n = cov.shape[1]
    step = 256
    last = cov.shape[0] // T
    small = pl.BlockSpec((8, T), lambda i: (0, 0))
    out = jax.ShapeDtypeStruct((T + 8, n), F32)
    return pl.pallas_call(
        row_edges_body,
        grid=(n // step,),
        in_specs=[
            pl.BlockSpec((2 * T, step), lambda i: (0, i)),
            pl.BlockSpec((2 * T, step), lambda i: (last // 2 - 1, i)),
            pl.BlockSpec((T, step), lambda i: (0, i)),
            pl.BlockSpec((T, step), lambda i: (last - 1, i)),
            small,
            small,
            small,
        ],
        out_specs=[pl.BlockSpec((T + 8, step), lambda i: (0, i))] * 2,
        out_shape=[out, out],
        scratch_shapes=[pltpu.VMEM((2, 7, T, T), F32)],
        compiler_params=cp(),
        name="row_edges",
    )(cov, cov, noise, noise, k, u, w)


def col_edges_body(pleft, pright, qleft, qright, upl, upr, dnl, dnr, k, u, w, cw, left, right):
    cols = columns(seven(k[...], u[...], w[...]))
    ck, cu, cv = cw[0:8, :], cw[8:16, :], cw[16:24, :]
    v = seven(ck, cu, cv)
    zero = jnp.zeros((T, T), F32)
    for x in range(8):
        e = [spread(cols, j, x) for j in range(7)]
        for p, q, up, dn, out, h, near, far, side in (
            (pleft, qleft, upl, dnl, left, 0, tile(0), tile(1), 1),
            (pright, qright, upr, dnr, right, 7, tile(1), tile(0), 2),
        ):
            vh = [a[h : h + 1, :] for a in v]
            mid = p[tile(x), near]
            low = 2.0 * up[...] if x == 0 else p[tile(x - 1), near]
            high = 2.0 * dn[...] if x == 7 else p[tile(x + 1), near]
            value = q[tile(x), :] + full(mid, low, high, e, 0)
            value = value + own(mid, vh, 1) + off(p[tile(x), far], vh, side, 1)
            out[tile(x), 0:T] = mid
            out[tile(x), T : 2 * T] = value
    for out, h in ((left, 0), (right, 7)):
        out[8 * T : 8 * T + 8, :] = jnp.zeros((8, 2 * T), F32)
        out[8 * T : 8 * T + 1, 0:T] = ck[h : h + 1, :]
        out[8 * T : 8 * T + 1, T : 2 * T] = cu[h : h + 1, :]


def col_edges(cov, noise, up_p, dn_p, k, u, w, cw):
    rows, n = cov.shape
    last = n // T - 1
    one = lambda i, j: pl.BlockSpec((T, T), lambda s: (i, j))
    small = pl.BlockSpec((8, T), lambda s: (0, 0))
    out = jax.ShapeDtypeStruct((rows + 8, 2 * T), F32)
    return pl.pallas_call(
        col_edges_body,
        grid=(1,),
        in_specs=[
            pl.BlockSpec((rows, 2 * T), lambda s: (0, 0)),
            pl.BlockSpec((rows, 2 * T), lambda s: (0, n // (2 * T) - 1)),
            pl.BlockSpec((rows, T), lambda s: (0, 0)),
            pl.BlockSpec((rows, T), lambda s: (0, last)),
            one(0, 0),
            one(0, last),
            one(0, 0),
            one(0, last),
            small,
            small,
            small,
            pl.BlockSpec((24, T), lambda s: (0, 0)),
        ],
        out_specs=[pl.BlockSpec((rows + 8, 2 * T), lambda s: (0, 0))] * 2,
        out_shape=[out, out],
        compiler_params=cp(),
        name="col_edges",
    )(cov, cov, noise, noise, up_p, up_p, dn_p, dn_p, k, u, w, cw)


def block_body(p_hbm, q_hbm, up, dn, k, u, w, cw, out_hbm, pe, fe, qo, wide, v_s, sem_p, sem_q, sem_o):
    n = 8 * T

    def load_p(x):
        return pltpu.make_async_copy(p_hbm.at[tile(x), :], pe.at[pl.ds((x + 1) * T, T), pl.ds(T, n)], sem_p.at[x])

    def load_q(x):
        return pltpu.make_async_copy(q_hbm.at[tile(x), :], qo.at[tile(x), :], sem_q.at[x])

    def save(x):
        return pltpu.make_async_copy(qo.at[tile(x), :], out_hbm.at[tile(x), :], sem_o.at[x])

    halo_u = pltpu.make_async_copy(up, pe.at[pl.ds(0, T), pl.ds(T, n)], sem_p.at[8])
    halo_d = pltpu.make_async_copy(dn, pe.at[pl.ds(9 * T, T), pl.ds(T, n)], sem_p.at[9])
    halo_u.start()
    for x in range(8):
        load_p(x).start()
        load_q(x).start()
    halo_d.start()
    pe[:, 0:T] = jnp.zeros((10 * T, T), F32)
    pe[:, 9 * T : 10 * T] = jnp.zeros((10 * T, T), F32)
    fe[:, 0:T] = jnp.zeros((10 * T, T), F32)
    fe[:, 9 * T : 10 * T] = jnp.zeros((10 * T, T), F32)
    fe[0:T, T : 9 * T] = jnp.zeros((T, n), F32)
    fe[9 * T : 10 * T, T : 9 * T] = jnp.zeros((T, n), F32)
    cols = columns(seven(k[...], u[...], w[...]))
    v = seven(cw[0:8, :], cw[8:16, :], cw[16:24, :])
    for x in range(8):
        for j in range(7):
            wide[x, j] = spread(cols, j, x)
            v_s[x, j] = jnp.broadcast_to(v[j][x : x + 1, :], (8, T))

    def apply(src, x, h):
        e = [wide[x, j] for j in range(7)]
        vh = [v_s[h, j, 0:1, :] for j in range(7)]
        row = lambda i: pl.ds(pl.multiple_of(i * T, T), T)
        mid = src[row(x + 1), row(h + 1)]
        a = full(mid, src[row(x), row(h + 1)], src[row(x + 2), row(h + 1)], e, 0)
        b = full(mid, src[row(x + 1), row(h)], src[row(x + 1), row(h + 2)], vh, 1)
        return mid, a + b

    def first(x):
        @pl.loop(0, 8)
        def _(h):
            _, value = apply(pe, x, h)
            fe[pl.ds((x + 1) * T, T), at_tile(h + 1)] = value + qo[tile(x), at_tile(h)]

    def second(x):
        @pl.loop(0, 8)
        def _(h):
            mid, value = apply(fe, x, h)
            qo[tile(x), at_tile(h)] = pe[pl.ds((x + 1) * T, T), at_tile(h + 1)] + STEP * mid + SECOND * value

    halo_u.wait()
    load_p(0).wait()
    for x in range(9):
        if x < 8:
            if x < 7:
                load_p(x + 1).wait()
            else:
                halo_d.wait()
            load_q(x).wait()
            first(x)
        if x > 0:
            second(x - 1)
            save(x - 1).start()
    for x in range(8):
        save(x).wait()


def block(cov, noise, up_p, dn_p, k, u, w, cw):
    return pl.pallas_call(
        block_body,
        in_specs=[hbm(), hbm(), hbm(), hbm(), vmem(), vmem(), vmem(), vmem()],
        out_specs=hbm(),
        out_shape=jax.ShapeDtypeStruct(cov.shape, F32),
        scratch_shapes=[
            pltpu.VMEM((10 * T, 10 * T), F32),
            pltpu.VMEM((10 * T, 10 * T), F32),
            pltpu.VMEM((8 * T, 8 * T), F32),
            pltpu.VMEM((8, 7, T, T), F32),
            pltpu.VMEM((8, 7, 8, T), F32),
            pltpu.SemaphoreType.DMA((10,)),
            pltpu.SemaphoreType.DMA((8,)),
            pltpu.SemaphoreType.DMA((8,)),
        ],
        compiler_params=cp(),
        name="block",
    )(cov, noise, up_p, dn_p, k, u, w, cw)


def row_halo_body(o_in, p, up, dn, gu, gd, k, u, w, cw, o_out, wide):
    s = pl.program_id(0)
    cols = columns(seven(k[...], u[...], w[...]))
    v = seven(cw[0:8, :], cw[8:16, :], cw[16:24, :])

    def side(x, xp, g, toward, back):
        beside = seven(
            jnp.broadcast_to(g[T : T + 1, 0:T], (8, T)), jnp.broadcast_to(g[T : T + 1, T : 2 * T], (8, T)), jnp.zeros((8, T), F32)
        )
        theirs = columns(beside)
        for j in (toward, 4, 6):
            wide[0, j] = spread(cols, j, x)
        for j in (back, 4, 6):
            wide[1, j] = spread(theirs, j, 0)
        e = [wide[0, j] for j in range(7)]
        f = [wide[1, j] for j in range(7)]
        zero = jnp.zeros((T, T), F32)
        for h in range(8):
            vh = [a[h : h + 1, :] for a in v]
            low = xp[:, tile(h - 1)] if h > 0 else zero
            high = xp[:, tile(h + 1)] if h < 7 else zero
            value = g[0:T, tile(h)] + off(p[:, tile(h)], f, back, 0) + full(xp[:, tile(h)], low, high, vh, 1)
            o_out[:, tile(h)] = o_in[:, tile(h)] + SECOND * off(value, e, toward, 0)

    @pl.when(s == 0)
    def _():
        side(0, up, gu, 2, 1)

    @pl.when(s == 1)
    def _():
        side(7, dn, gd, 1, 2)


def row_halo(out, cov, up_p, dn_p, gu, gd, k, u, w, cw):
    n = cov.shape[1]
    whole = lambda r, c: pl.BlockSpec((r, c), lambda s: (0, 0))
    edge = pl.BlockSpec((T, n), lambda s: (7 * s, 0))
    return pl.pallas_call(
        row_halo_body,
        grid=(2,),
        in_specs=[edge, edge, whole(T, n), whole(T, n), whole(T + 8, n), whole(T + 8, n), whole(8, T), whole(8, T), whole(8, T), whole(24, T)],
        out_specs=edge,
        out_shape=jax.ShapeDtypeStruct(out.shape, F32),
        scratch_shapes=[pltpu.VMEM((2, 7, T, T), F32)],
        input_output_aliases={0: 0},
        compiler_params=cp(),
        name="row_halo",
    )(out, cov, up_p, dn_p, gu, gd, k, u, w, cw)


def col_halo_body(o_in, p, yl, yr, k, u, w, cw, o_out, d):
    s = pl.program_id(0)
    cols = columns(seven(k[...], u[...], w[...]))
    v = seven(cw[0:8, :], cw[8:16, :], cw[16:24, :])
    zero = jnp.zeros((T, T), F32)

    def side(y, h, h2, near, far, mine, toward, back):
        tail = pl.ds(8 * T, 1)
        beside = seven(
            jnp.broadcast_to(y[tail, 0:T], (8, T)), jnp.broadcast_to(y[tail, T : 2 * T], (8, T)), jnp.zeros((8, T), F32)
        )
        f = [a[0:1, :] for a in beside]
        vh = [a[h : h + 1, :] for a in v]
        v2 = [a[h2 : h2 + 1, :] for a in v]
        for x in range(8):
            d[tile(x), :] = off(y[tile(x), 0:T], vh, toward, 1)
        for x in range(8):
            e = [spread(cols, j, x) for j in range(7)]
            mid = d[tile(x), :]
            low = d[tile(x - 1), :] if x > 0 else zero
            high = d[tile(x + 1), :] if x < 7 else zero
            beyond = y[tile(x), T : 2 * T] + off(p[tile(x), mine], f, back, 1)
            value = own(mid, vh, 1) + full(mid, low, high, e, 0) + off(beyond, vh, toward, 1)
            o_out[tile(x), near] = o_in[tile(x), near] + STEP * mid + SECOND * value
            o_out[tile(x), far] = o_in[tile(x), far] + SECOND * off(mid, v2, toward, 1)

    @pl.when(s == 0)
    def _():
        side(yl, 0, 1, tile(0), tile(1), tile(0), 2, 1)

    @pl.when(s == 1)
    def _():
        side(yr, 7, 6, tile(1), tile(0), tile(0), 1, 2)


def col_halo(out, cov, yl, yr, k, u, w, cw):
    rows, n = cov.shape
    whole = lambda r, c: pl.BlockSpec((r, c), lambda s: (0, 0))
    edge = pl.BlockSpec((rows, 2 * T), lambda s: (0, (n // (2 * T) - 1) * s))
    return pl.pallas_call(
        col_halo_body,
        grid=(2,),
        in_specs=[
            edge,
            pl.BlockSpec((rows, T), lambda s: (0, (n // T - 1) * s)),
            whole(rows + 8, 2 * T),
            whole(rows + 8, 2 * T),
            whole(8, T),
            whole(8, T),
            whole(8, T),
            whole(24, T),
        ],
        out_specs=edge,
        out_shape=jax.ShapeDtypeStruct(out.shape, F32),
        scratch_shapes=[pltpu.VMEM((rows, T), F32)],
        input_output_aliases={0: 0},
        compiler_params=cp(),
        name="col_halo",
    )(out, cov, yl, yr, k, u, w, cw)


@functools.cache
def weight_route(n):
    def place(r, c):
        half = n // 2
        return (2 * (c // half) + r // half, (c % half) // 2, r % half, c % 2)

    def far(a, b):
        ring = lambda d, size: min(d % size, -d % size)
        return ring(a[0] - b[0], 4) + ring(a[1] - b[1], max(n // 4, 1)) + ring(a[2] - b[2], n // 2) + 0.5 * (a[3] != b[3])

    pairs = []
    for c in range(n):
        cost = [[far(place(r, c), place(c, f)) for f in range(n)] for r in range(n)]
        for limit in sorted({x for row in cost for x in row}):
            taken = {}

            def find(r, seen):
                for f in sorted(range(n), key=lambda f: cost[r][f]):
                    if cost[r][f] <= limit and f not in seen:
                        seen.add(f)
                        if f not in taken or find(taken[f], seen):
                            taken[f] = r
                            return True
                return False

            if all(find(r, set()) for r in range(n)):
                break
        pairs += [(c * n + f, r * n + c) for f, r in taken.items()]
    return sorted(pairs)


def per_device(cov, noise, k, u, w):
    rows = lax.axis_size("row")
    cols = lax.axis_size("col")
    n0, n1 = cov.shape
    up = lambda n: [(i, i + 1) for i in range(n - 1)]
    down = lambda n: [(i + 1, i) for i in range(n - 1)]
    from_up = lambda a: lax.ppermute(a, "row", up(rows))
    from_dn = lambda a: lax.ppermute(a, "row", down(rows))

    up_p = from_up(cov[n0 - T :, :])
    dn_p = from_dn(cov[:T, :])
    cw = lax.ppermute(jnp.concatenate([k, u, w], axis=0), ("row", "col"), weight_route(rows))
    top, bottom = row_edges(cov, noise, k, u, w)
    gu = from_up(bottom)
    gd = from_dn(top)
    up_p, dn_p, _, _ = lax.optimization_barrier((up_p, dn_p, top, bottom))
    left, right = col_edges(cov, noise, up_p, dn_p, k, u, w, cw)
    yl = lax.ppermute(right, "col", up(cols))
    yr = lax.ppermute(left, "col", down(cols))
    out = block(cov, noise, up_p, dn_p, k, u, w, cw)
    out = row_halo(out, cov, up_p, dn_p, gu, gd, k, u, w, cw)
    return col_halo(out, cov, yl, yr, k, u, w, cw)


def solution(mesh):
    return jax.shard_map(
        per_device,
        mesh=mesh,
        in_specs=(P("row", "col"), P("row", "col"), P("row", None), P("row", None), P("row", None)),
        out_specs=P("row", "col"),
        check_vma=False,
    )
```

time: 211 us -> 77.7 us (0.37)
  the two profiles are of different devices: /device:TPU:25 before, /device:TPU:6 now
where the time goes in v1:
time: 77.7 us; the launch traced here: 77.2 us
  Pallas kernels  38.5 us (50%)
  starting transfers between devices  32.1 us (41%)
  local copies, waits for them, and re-layouts  5.57 us (7%)
    pallas_call x1, Pallas kernels, block(): pl.pallas_call(block_body, in_specs=[hbm(), hbm(), hbm(), hbm(), vmem(),...  18 us
    ppermute x2, starting transfers between devices, per_device(): from_dn = lambda a: lax.ppermute(a, 'row', down(rows))  12.8 us
    pallas_call x1, Pallas kernels, col_halo(): pl.pallas_call(col_halo_body, grid=(2,), in_specs=[edge, pl.BlockSpec((ro...  8.1 us
    ppermute x1, starting transfers between devices, per_device(): yr = lax.ppermute(left, 'col', down(cols))  6.74 us
    ppermute x2, starting transfers between devices, per_device(): from_up = lambda a: lax.ppermute(a, 'row', up(rows))  6.49 us
    pallas_call x1, Pallas kernels, col_edges(): pl.pallas_call(col_edges_body, grid=(1,), in_specs=[pl.BlockSpec((rows, 2...  4.87 us
    pallas_call x1, Pallas kernels, row_halo(): pl.pallas_call(row_halo_body, grid=(2,), in_specs=[edge, edge, whole(T, n...  4.3 us
    unnamed x16, local copies, waits for them, and re-layouts  4.27 us
  transfers between devices with their start and end apart: 7, of which 0 were waited for; matrix products, arithmetic and copies ran while one was open for 1% of the time, Pallas kernels for 33%

profile of v1, /device:TPU:6, one launch (start us, length us, event | category | flops | bytes accessed | tf_op | source)
XLA Modules:
  0.0 77.2 jit_solution(4689910481062636316)
XLA Ops:
  0.0 1.3 %fusion = (f32[128,1024]{1,0:T(8,128)S(1)}, f32[128,1024]{1,0:T(8,128)S(1)}) fusion(f32[1024,1024]{1,0:T(8,128)} %p.3), kind=kLoop, calls=%fused_computation.1 | loop fusion | bytes 2097152 | tf_op jit(solution)/shard_map/slice | solution.py:439
  1.3 3.8 %collective-permute-start = (f32[128,1024]{1,0:T(8,128)S(1)}, f32[128,1024]{1,0:T(8,128)S(1)}, u32[]{:S(2)}, u32[]{:S(2)}) collective-permute-start(f32[128,1024]{1,0:T(8,128)S(1)} %get-tuple-element.18), channel_id=1, source_target_pairs={{0,16},{16,32},{32,48},{48,64},{64,80},{80,96},{96,112},{112,128},... | collective-permute-start | bytes 1572872 | tf_op jit(solution)/shard_map/ppermute | solution.py:435
  5.1 6.1 %collective-permute-start.1 = (f32[128,1024]{1,0:T(8,128)S(1)}, f32[128,1024]{1,0:T(8,128)S(1)}, u32[]{:S(2)}, u32[]{:S(2)}) collective-permute-start(f32[128,1024]{1,0:T(8,128)S(1)} %get-tuple-element.17), channel_id=1, source_target_pairs={{16,0},{32,16},{48,32},{64,48},{80,64},{96,80},{112,96},{128,112},... | collective-permute-start | bytes 1572872 | tf_op jit(solution)/shard_map/ppermute | solution.py:436
  11.3 0.7 pad_maximum_fusion
  12.0 3.7 %collective-permute-start.2 = (f32[24,128]{1,0:T(8,128)S(1)}, f32[24,128]{1,0:T(8,128)S(1)}, u32[]{:S(2)}, u32[]{:S(2)}) collective-permute-start(f32[24,128]{1,0:T(8,128)S(1)} %pad_maximum_fusion), channel_id=1, source_target_pairs={{0,240},{1,224},{2,176},{3,96},{4,48},{5,32},{6,64},{7,80},{8,192}... | collective-permute-start | bytes 36872 | tf_op jit(solution)/shard_map/ppermute | solution.py:440
  15.7 0.0 copy-start
  15.7 2.2 %copy-done = f32[1024,1024]{1,0:T(8,128)S(1)} copy-done((f32[1024,1024]{1,0:T(8,128)S(1)}, f32[1024,1024]{1,0:T(8,128)}, u32[]{:S(2)}) %copy-start) | copy-done | bytes 4194328
  17.9 0.0 copy-start.2
  17.9 0.7 copy-done.2
  18.6 0.0 copy-start.4
  18.6 0.7 copy-done.4
  19.2 0.0 copy-start.6
  19.2 0.7 copy-done.6
  19.9 3.3 %row_edges.1 = (f32[136,1024]{1,0:T(8,128)S(1)}, f32[136,1024]{1,0:T(8,128)S(1)}) custom-call(f32[1024,1024]{1,0:T(8,128)S(1)} %copy-done, f32[1024,1024]{1,0:T(8,128)S(1)} %copy-done, f32[1024,1024]{1,0:T(8,128)} %qright.1, f32[1024,1024]{1,0:T(8,128)} %qright.1, f32[8,128]{1,0:T(8,128)S(1)} %copy-done.2, f32[8,128]{1,0:T(8,128)S(1)} %copy-done.4, ...), custom_call_target="tpu_custom_call" | custom-call | tf_op jit(solution)/shard_map/row_edges/pallas_call | solution.py:121
  23.2 0.0 collective-permute-done.up.upl.upr
  23.2 0.0 collective-permute-done.1.dn.dnl.dnr
  23.2 0.0 copy-start.1
  23.2 0.0 copy-start.3
  23.3 0.0 copy-start.5
  23.3 0.0 copy-start.7
  23.3 0.0 collective-permute-done.2.cw
  23.3 4.9 %col_edges.1 = (f32[1032,256]{1,0:T(8,128)S(1)}, f32[1032,256]{1,0:T(8,128)S(1)}) custom-call(f32[1024,1024]{1,0:T(8,128)} %p.3, f32[1024,1024]{1,0:T(8,128)} %p.3, f32[1024,1024]{1,0:T(8,128)} %qright.1, f32[1024,1024]{1,0:T(8,128)} %qright.1, f32[128,1024]{1,0:T(8,128)S(1)} %collective-permute-done.up.upl.upr, ...), custom_call_target="tpu_custom_call" | custom-call | tf_op jit(solution)/shard_map/col_edges/pallas_call | solution.py:172
  28.2 2.4 %collective-permute-start.5 = (f32[1032,256]{1,0:T(8,128)S(1)}, f32[1032,256]{1,0:T(8,128)S(1)}, u32[]{:S(2)}, u32[]{:S(2)}) collective-permute-start(f32[1032,256]{1,0:T(8,128)S(1)} %get-tuple-element.15), channel_id=1, source_target_pairs={{0,1},{1,2},{2,3},{3,4},{4,5},{5,6},{6,7},{7,8},{8,9},{9,10},{10,1... | collective-permute-start | bytes 3170312 | tf_op jit(solution)/shard_map/ppermute | solution.py:446
  30.6 6.7 %collective-permute-start.6 = (f32[1032,256]{1,0:T(8,128)S(1)}, f32[1032,256]{1,0:T(8,128)S(1)}, u32[]{:S(2)}, u32[]{:S(2)}) collective-permute-start(f32[1032,256]{1,0:T(8,128)S(1)} %get-tuple-element.16), channel_id=1, source_target_pairs={{1,0},{2,1},{3,2},{4,3},{5,4},{6,5},{7,6},{8,7},{9,8},{10,9},{11,1... | collective-permute-start | bytes 3170312 | tf_op jit(solution)/shard_map/ppermute | solution.py:447
  37.4 2.7 %collective-permute-start.3 = (f32[136,1024]{1,0:T(8,128)S(1)}, f32[136,1024]{1,0:T(8,128)S(1)}, u32[]{:S(2)}, u32[]{:S(2)}) collective-permute-start(f32[136,1024]{1,0:T(8,128)S(1)} %get-tuple-element.12), channel_id=1, source_target_pairs={{0,16},{16,32},{32,48},{48,64},{64,80},{80,96},{96,112},{112,128},... | collective-permute-start | bytes 1671176 | tf_op jit(solution)/shard_map/ppermute | solution.py:435
  40.0 6.7 %collective-permute-start.4 = (f32[136,1024]{1,0:T(8,128)S(1)}, f32[136,1024]{1,0:T(8,128)S(1)}, u32[]{:S(2)}, u32[]{:S(2)}) collective-permute-start(f32[136,1024]{1,0:T(8,128)S(1)} %get-tuple-element.11), channel_id=1, source_target_pairs={{16,0},{32,16},{48,32},{64,48},{80,64},{96,80},{112,96},{128,112},... | collective-permute-start | bytes 1671176 | tf_op jit(solution)/shard_map/ppermute | solution.py:436
  46.7 0.0 copy-done.1
  46.7 0.0 copy-done.3
  46.7 0.0 copy-done.5
  46.7 0.0 copy-done.7
  46.7 18.0 %block.1.o_in = f32[1024,1024]{1,0:T(8,128)} custom-call(f32[1024,1024]{1,0:T(8,128)S(1)} %copy-done.1, f32[1024,1024]{1,0:T(8,128)} %qright.1, f32[128,1024]{1,0:T(8,128)S(1)} %collective-permute-done.up.upl.upr, f32[128,1024]{1,0:T(8,128)S(1)} %collective-permute-done.1.dn.dnl.dnr, f32[8,128]{1,0:T(8,128)S(1)} %copy-done.3, f32[8,128]{1,0:T(8,128)S(1)} %copy-done.5, ...), custom_call_target="tpu_custom_call" | custom-call | tf_op jit(solution)/shard_map/block/pallas_call | solution.py:267
  64.7 0.0 collective-permute-done.3.gu
  64.7 0.0 collective-permute-done.4.gd
  64.8 4.3 %row_halo.1.o_in = f32[1024,1024]{1,0:T(8,128)} custom-call(f32[1024,1024]{1,0:T(8,128)} %block.1.o_in, f32[1024,1024]{1,0:T(8,128)} %p.3, f32[128,1024]{1,0:T(8,128)S(1)} %collective-permute-done.up.upl.upr, f32[128,1024]{1,0:T(8,128)S(1)} %collective-permute-done.1.dn.dnl.dnr, ...), custom_call_target="tpu_custom_call", output_to_operand_aliasing={{}: (0, {})} | custom-call | tf_op jit(solution)/shard_map/row_halo/pallas_call | solution.py:324
  69.1 0.0 collective-permute-done.5.yl
  69.1 0.0 collective-permute-done.6.yr
  69.1 8.1 %col_halo.1 = f32[1024,1024]{1,0:T(8,128)} custom-call(f32[1024,1024]{1,0:T(8,128)} %row_halo.1.o_in, f32[1024,1024]{1,0:T(8,128)} %p.3, f32[1032,256]{1,0:T(8,128)S(1)} %collective-permute-done.5.yl, f32[1032,256]{1,0:T(8,128)S(1)} %collective-permute-done.6.yr, f32[8,128]{1,0:T(8,128)S(1)} %copy-done.3, ...), custom_call_target="tpu_custom_call", output_to_operand_aliasing={{}: (0, {})} | custom-call | tf_op jit(solution)/shard_map/col_halo/pallas_call | solution.py:376
Async XLA Ops:
  1.3 21.9 %collective-permute-start = (f32[128,1024]{1,0:T(8,128)S(1)}, f32[128,1024]{1,0:T(8,128)S(1)}, u32[]{:S(2)}, u32[]{:S(2)}) collective-permute-start(f32[128,1024]{1,0:T(8,128)S(1)} %get-tuple-element.18), channel_id=1, source_target_pairs={{0,16},{16,32},{32,48},{48,64},{64,80},{80,96},{96,112},{112,128},... | collective-permute-start | bytes 1572872 | tf_op jit(solution)/shard_map/ppermute | solution.py:435
  5.1 18.1 %collective-permute-start.1 = (f32[128,1024]{1,0:T(8,128)S(1)}, f32[128,1024]{1,0:T(8,128)S(1)}, u32[]{:S(2)}, u32[]{:S(2)}) collective-permute-start(f32[128,1024]{1,0:T(8,128)S(1)} %get-tuple-element.17), channel_id=1, source_target_pairs={{16,0},{32,16},{48,32},{64,48},{80,64},{96,80},{112,96},{128,112},... | collective-permute-start | bytes 1572872 | tf_op jit(solution)/shard_map/ppermute | solution.py:436
  12.0 11.3 %collective-permute-start.2 = (f32[24,128]{1,0:T(8,128)S(1)}, f32[24,128]{1,0:T(8,128)S(1)}, u32[]{:S(2)}, u32[]{:S(2)}) collective-permute-start(f32[24,128]{1,0:T(8,128)S(1)} %pad_maximum_fusion), channel_id=1, source_target_pairs={{0,240},{1,224},{2,176},{3,96},{4,48},{5,32},{6,64},{7,80},{8,192}... | collective-permute-start | bytes 36872 | tf_op jit(solution)/shard_map/ppermute | solution.py:440
  15.7 2.2 %copy-start = (f32[1024,1024]{1,0:T(8,128)S(1)}, f32[1024,1024]{1,0:T(8,128)}, u32[]{:S(2)}) copy-start(f32[1024,1024]{1,0:T(8,128)} %p.3) | copy-start | bytes 12582916
  17.9 0.7 copy-start.2
  18.6 0.7 copy-start.4
  19.2 0.7 copy-start.6
  23.2 23.5 %copy-start.1 = (f32[1024,1024]{1,0:T(8,128)S(1)}, f32[1024,1024]{1,0:T(8,128)}, u32[]{:S(2)}) copy-start(f32[1024,1024]{1,0:T(8,128)} %p.3) | copy-start | bytes 12582916
  23.2 23.5 %copy-start.3 = (f32[8,128]{1,0:T(8,128)S(1)}, f32[8,128]{1,0:T(8,128)}, u32[]{:S(2)}) copy-start(f32[8,128]{1,0:T(8,128)} %k.9) | copy-start | bytes 12292
  23.3 23.5 %copy-start.5 = (f32[8,128]{1,0:T(8,128)S(1)}, f32[8,128]{1,0:T(8,128)}, u32[]{:S(2)}) copy-start(f32[8,128]{1,0:T(8,128)} %u.9) | copy-start | bytes 12292
  23.3 23.5 %copy-start.7 = (f32[8,128]{1,0:T(8,128)S(1)}, f32[8,128]{1,0:T(8,128)}, u32[]{:S(2)}) copy-start(f32[8,128]{1,0:T(8,128)} %w.9) | copy-start | bytes 12292
  28.2 40.9 %collective-permute-start.5 = (f32[1032,256]{1,0:T(8,128)S(1)}, f32[1032,256]{1,0:T(8,128)S(1)}, u32[]{:S(2)}, u32[]{:S(2)}) collective-permute-start(f32[1032,256]{1,0:T(8,128)S(1)} %get-tuple-element.15), channel_id=1, source_target_pairs={{0,1},{1,2},{2,3},{3,4},{4,5},{5,6},{6,7},{7,8},{8,9},{9,10},{10,1... | collective-permute-start | bytes 3170312 | tf_op jit(solution)/shard_map/ppermute | solution.py:446
  30.6 38.4 %collective-permute-start.6 = (f32[1032,256]{1,0:T(8,128)S(1)}, f32[1032,256]{1,0:T(8,128)S(1)}, u32[]{:S(2)}, u32[]{:S(2)}) collective-permute-start(f32[1032,256]{1,0:T(8,128)S(1)} %get-tuple-element.16), channel_id=1, source_target_pairs={{1,0},{2,1},{3,2},{4,3},{5,4},{6,5},{7,6},{8,7},{9,8},{10,9},{11,1... | collective-permute-start | bytes 3170312 | tf_op jit(solution)/shard_map/ppermute | solution.py:447
  37.4 27.4 %collective-permute-start.3 = (f32[136,1024]{1,0:T(8,128)S(1)}, f32[136,1024]{1,0:T(8,128)S(1)}, u32[]{:S(2)}, u32[]{:S(2)}) collective-permute-start(f32[136,1024]{1,0:T(8,128)S(1)} %get-tuple-element.12), channel_id=1, source_target_pairs={{0,16},{16,32},{32,48},{48,64},{64,80},{80,96},{96,112},{112,128},... | collective-permute-start | bytes 1671176 | tf_op jit(solution)/shard_map/ppermute | solution.py:435
  40.0 24.7 %collective-permute-start.4 = (f32[136,1024]{1,0:T(8,128)S(1)}, f32[136,1024]{1,0:T(8,128)S(1)}, u32[]{:S(2)}, u32[]{:S(2)}) collective-permute-start(f32[136,1024]{1,0:T(8,128)S(1)} %get-tuple-element.11), channel_id=1, source_target_pairs={{16,0},{32,16},{48,32},{64,48},{80,64},{96,80},{112,96},{128,112},... | collective-permute-start | bytes 1671176 | tf_op jit(solution)/shard_map/ppermute | solution.py:436

commit v2 on v0

v2 whole, which is shorter than its diff:
```python
import functools

import jax
import jax.numpy as jnp
from jax import lax
from jax.experimental import pallas as pl
from jax.experimental.pallas import tpu as pltpu
from jax.sharding import PartitionSpec as P

T = 128
N = 8 * T
F32 = jnp.float32
BF16 = jnp.bfloat16
STEP = 0.1
SECOND = 0.5 * STEP * STEP


def seven(kappa, flow_x, flow_y):
    edge = (4.0 / 6.0) * kappa
    corner = kappa / 6.0
    at = lax.broadcasted_iota(jnp.int32, kappa.shape, 1)

    def from_above(v):
        return jnp.where(at == 0, 0.0, pltpu.roll(v, 1, 1))

    def from_below(v):
        return jnp.where(at == T - 1, 0.0, pltpu.roll(v, T - 1, 1))

    return [
        (-20.0 / 6.0) * kappa,
        edge - 0.5 * flow_x,
        edge + 0.5 * flow_x,
        from_above(edge - 0.5 * flow_y),
        from_above(corner),
        from_below(edge + 0.5 * flow_y),
        from_below(corner),
    ]


def columns(lists):
    rows = list(lists)
    have = 8 * len(rows)
    if have < T:
        rows.append(jnp.zeros((T - have, T), F32))
    return jnp.concatenate(rows, axis=0).T


def spread(cols, j, x):
    return jnp.broadcast_to(cols[:, 8 * j + x : 8 * j + x + 1], (T, T))


def shifted(up, down, axis):
    return pltpu.roll(up, T - 1, axis) + pltpu.roll(down, 1, axis)


def full(mid, low, high, w, axis):
    both = low + high
    return w[0] * mid + w[1] * high + w[2] * low + shifted(w[3] * mid + w[4] * both, w[5] * mid + w[6] * both, axis)


def off(value, w, side, axis):
    return w[side] * value + shifted(w[4] * value, w[6] * value, axis)


def split(value):
    high = value.astype(BF16)
    return high, (value - high.astype(F32)).astype(BF16)


def times(value, weights):
    (vh, vl), (wh, wl) = split(value), weights
    dot = lambda a, b: jnp.dot(a, b, preferred_element_type=F32)
    return dot(vh, wh) + dot(vl, wh) + dot(vh, wl)


def right_factor(kuw, h, which):
    k, u, w = (v[h : h + 1, :] for v in kuw)
    i = lax.broadcasted_iota(jnp.int32, (T, T), 0)
    j = lax.broadcasted_iota(jnp.int32, (T, T), 1)
    edge = (4.0 / 6.0) * k
    if which == "own":
        mid, up, down = (-20.0 / 6.0) * k, edge - 0.5 * w, edge + 0.5 * w
    else:
        mid = edge - 0.5 * u if which == "next" else edge + 0.5 * u
        up = down = k / 6.0
    return jnp.where(i == j, mid, jnp.where(i == j + 1, up, jnp.where(i == j - 1, down, 0.0)))


def tables(ref):
    return ref[0:8, :], ref[8:16, :], ref[16:24, :]


def tile(i):
    return slice(i * T, (i + 1) * T)


def at_tile(i):
    return pl.ds(pl.multiple_of(i * T, T), T)


def call(body, out, scratch, ins, name, us):
    shapes = [jax.ShapeDtypeStruct(s, F32) for s, _ in out]
    specs = [space for _, space in out]
    return pl.pallas_call(
        body,
        in_specs=ins,
        out_specs=specs,
        out_shape=shapes,
        scratch_shapes=scratch,
        compiler_params=pltpu.CompilerParams(vmem_limit_bytes=40 << 20),
        cost_estimate=pl.CostEstimate(flops=us * 10**9, transcendentals=0, bytes_accessed=us * 3 * 10**6),
        name=name,
    )


VMEM = pl.BlockSpec(memory_space=pltpu.VMEM)
HBM = pl.BlockSpec(memory_space=pltpu.HBM)
DMA = pltpu.SemaphoreType.DMA
copy = pltpu.make_async_copy


def pack_body(p, k, u, w, left, right, kuw, sem):
    moves = [copy(v, kuw.at[pl.ds(8 * i, 8), :], sem.at[i]) for i, v in enumerate((k, u, w))]
    moves += [copy(p.at[:, pl.ds(7 * T * s, T)], out, sem.at[3 + s]) for s, out in enumerate((left, right))]
    for m in moves:
        m.start()
    for m in moves:
        m.wait()


def pack(cov, k, u, w):
    edge = ((N, T), VMEM)
    return call(pack_body, [edge, edge, ((24, T), VMEM)], [DMA((5,))], [HBM] * 4, "pack", 1)(cov, k, u, w)


def row_edges_body(p, q, kuw, top, bottom, wide, pb, sem):
    moves = []
    for i, out in enumerate((top, bottom)):
        moves.append(copy(p.at[pl.ds(7 * T * i, T), :], out.at[pl.ds(0, T), :], sem.at[3 * i]))
        moves.append(copy(q.at[pl.ds(7 * T * i, T), :], out.at[pl.ds(T, T), :], sem.at[3 * i + 1]))
        moves.append(copy(p.at[pl.ds(T + 5 * T * i, T), :], pb.at[i], sem.at[3 * i + 2]))
    for m in moves:
        m.start()
    cols = columns(seven(*tables(kuw)))
    for x in range(8):
        for j in range(7):
            wide[x, j] = spread(cols, j, x)
    for i, x, side, out in ((0, 0, 1, top), (1, 7, 2, bottom)):
        out[2 * T : 2 * T + 8, :] = jnp.zeros((8, N), F32)
        out[2 * T : 2 * T + 1, 0:T] = kuw[x : x + 1, :]
        out[2 * T : 2 * T + 1, T : 2 * T] = kuw[8 + x : 9 + x, :]
        for m in moves[3 * i : 3 * i + 3]:
            m.wait()

        @pl.loop(0, 8, unroll=8)
        def _(h):
            lanes = at_tile(h)
            m, n = out[0:T, lanes], pb[i, :, lanes]
            e = [wide[x, j] for j in range(7)]
            both = shifted(e[3] * m + e[4] * n, e[5] * m + e[6] * n, 0)
            out[T : 2 * T, lanes] = out[T : 2 * T, lanes] + (e[0] * m + e[side] * n + both)


def row_edges(cov, noise, kuw):
    edge = ((2 * T + 8, N), VMEM)
    scratch = [pltpu.VMEM((2, T, N), F32), DMA((6,))]
    return call(row_edges_body, [edge, edge, ((8, 7, T, T), VMEM)], scratch, [HBM, HBM, VMEM], "row_edges", 2)(cov, noise, kuw)


def row_finish_body(top, bottom, yl, yr, cw, top_out, bottom_out):
    v = seven(*tables(cw))
    for i, (src, out) in enumerate(((top, top_out), (bottom, bottom_out))):
        rows = pl.ds(7 * T * i, T)
        out[0:T, :] = src[0:T, :]
        out[2 * T : 2 * T + 8, :] = src[2 * T : 2 * T + 8, :]
        for h in range(8):
            low = 2.0 * yl[rows, :] if h == 0 else src[0:T, tile(h - 1)]
            high = 2.0 * yr[rows, :] if h == 7 else src[0:T, tile(h + 1)]
            term = full(src[0:T, tile(h)], low, high, [a[h : h + 1, :] for a in v], 1)
            out[T : 2 * T, tile(h)] = src[T : 2 * T, tile(h)] + term


def row_finish(top, bottom, yl, yr, cw):
    edge = ((2 * T + 8, N), VMEM)
    return call(row_finish_body, [edge, edge], [], [VMEM] * 5, "row_finish", 2)(top, bottom, yl, yr, cw)


def col_edges_body(p, q, wide, cw, left, right, pb, qb, sem):
    moves = []
    for s in range(2):
        moves.append(copy(p.at[:, pl.ds(6 * T * s, 2 * T)], pb.at[s], sem.at[2 * s]))
        moves.append(copy(q.at[:, pl.ds(7 * T * s, T)], qb.at[s], sem.at[2 * s + 1]))
    for m in moves:
        m.start()
    kuw = tables(cw)
    zero = jnp.zeros((T, T), F32)
    for s, h, out in ((0, 0, left), (1, 7, right)):
        out[N : N + 8, :] = jnp.zeros((8, T), F32)
        for i in range(2):
            out[N + i : N + i + 1, :] = kuw[i][h : h + 1, :]
        near, far = right_factor(kuw, h, "own"), right_factor(kuw, h, "before" if s else "next")
        factor = split(jnp.concatenate([far, near] if s else [near, far], axis=0))
        moves[2 * s].wait()
        moves[2 * s + 1].wait()
        mine = tile(s)
        out[0:N, :] = times(pb[s], factor)
        for x in range(8):
            e = [wide[x, j] for j in range(7)]
            low = zero if x == 0 else pb[s, tile(x - 1), mine]
            high = zero if x == 7 else pb[s, tile(x + 1), mine]
            out[tile(x), :] = out[tile(x), :] + (qb[s, tile(x), :] + full(pb[s, tile(x), mine], low, high, e, 0))


def col_edges(cov, noise, wide, cw):
    edge = ((N + 8, T), VMEM)
    scratch = [pltpu.VMEM((2, N, 2 * T), F32), pltpu.VMEM((2, N, T), F32), DMA((4,))]
    return call(col_edges_body, [edge, edge], scratch, [HBM, HBM] + [VMEM] * 2, "col_edges", 3)(cov, noise, wide, cw)


def block_body(p_hbm, q_hbm, yl, yr, wide, cw, o, pe, fe, v_s, sem_p, sem_q):
    def load_p(x):
        return copy(p_hbm.at[tile(x), :], pe.at[pl.ds((x + 1) * T, T), pl.ds(T, N)], sem_p.at[x])

    def load_q(x):
        return copy(q_hbm.at[tile(x), :], o.at[tile(x), :], sem_q.at[x])

    for x in range(8):
        load_p(x).start()
        load_q(x).start()
    inner = slice(T, 9 * T)
    pe[inner, 0:T] = yl[...]
    pe[inner, 9 * T : 10 * T] = yr[...]
    fe[inner, 0:T] = jnp.zeros((N, T), F32)
    fe[inner, 9 * T : 10 * T] = jnp.zeros((N, T), F32)
    for r in (pe, fe):
        r[0:T, inner] = jnp.zeros((T, N), F32)
        r[9 * T : 10 * T, inner] = jnp.zeros((T, N), F32)
    v = seven(*tables(cw))
    for x in range(8):
        for j in range(7):
            v_s[0, x, j] = jnp.broadcast_to(v[j][x : x + 1, :], (8, T))
        v_s[1, x, 0] = jnp.broadcast_to(v[0][x : x + 1, :] + STEP / SECOND, (8, T))
        for j in range(1, 7):
            v_s[1, x, j] = v_s[0, x, j]

    def apply(src, x, h, stage):
        e = [wide[x, j] for j in range(7)]
        v = [v_s[stage, h, j, 0:1, :] for j in range(7)]
        rows = pl.ds((x + 1) * T, T)
        mid, low, high = (src[rows, at_tile(h + i)] for i in (1, 0, 2))
        both = low + high
        value = (e[0] + v[0]) * mid + v[1] * high + v[2] * low
        value = value + shifted(v[3] * mid + v[4] * both, v[5] * mid + v[6] * both, 1)
        low, high = (src[pl.ds((x + i) * T, T), at_tile(h + 1)] for i in (0, 2))
        both = low + high
        value = value + e[1] * high + e[2] * low
        return value + shifted(e[3] * mid + e[4] * both, e[5] * mid + e[6] * both, 0)

    def first(x):
        @pl.loop(0, 8, unroll=8)
        def _(h):
            fe[pl.ds((x + 1) * T, T), at_tile(h + 1)] = o[tile(x), at_tile(h)] + apply(pe, x, h, 0)

    def second(x):
        @pl.loop(0, 8, unroll=8)
        def _(h):
            o[tile(x), at_tile(h)] = pe[pl.ds((x + 1) * T, T), at_tile(h + 1)] + SECOND * apply(fe, x, h, 1)

    load_p(0).wait()
    for x in range(9):
        if x < 8:
            if x < 7:
                load_p(x + 1).wait()
            load_q(x).wait()
            first(x)
        if x > 0:
            second(x - 1)


def block(cov, noise, yl, yr, wide, cw):
    scratch = [
        pltpu.VMEM((10 * T, 10 * T), F32),
        pltpu.VMEM((10 * T, 10 * T), F32),
        pltpu.VMEM((2, 8, 7, 8, T), F32),
        DMA((8,)),
        DMA((8,)),
    ]
    return call(block_body, [((N, N), VMEM)], scratch, [HBM, HBM] + [VMEM] * 4, "block", 16)(cov, noise, yl, yr, wide, cw)[0]


def halo_body(o, top, bottom, left, right, ru, rd, fl, fr, wide, cw, out, cb, rb, d, theirs, sem):
    inner = copy(o.at[pl.ds(2 * T, 4 * T), pl.ds(T, 6 * T)], out.at[pl.ds(2 * T, 4 * T), pl.ds(T, 6 * T)], sem.at[0])
    inner.start()
    saves = [inner]
    v = seven(*tables(cw))
    for s, (f, mine, h, toward, back) in enumerate(((fl, left, 0, 2, 1), (fr, right, 7, 1, 2))):
        spot = lambda i: jnp.broadcast_to(f[N + i : N + i + 1, :], (8, T))
        b = [a[0:1, :] for a in seven(spot(0), spot(1), jnp.zeros((8, T), F32))]
        vh = [a[h : h + 1, :] for a in v]
        for x in range(8):
            beside = f[tile(x), :] + off(mine[tile(x), :], b, back, 1)
            cb[s, tile(x), :] = o[tile(x), tile(h)] + SECOND * off(beside, vh, toward, 1)
        rows = pl.ds(2 * T, 4 * T)
        saves.append(copy(cb.at[s, rows, :], out.at[rows, pl.ds(7 * T * s, T)], sem.at[1 + s]))
        saves[-1].start()
    zero = jnp.zeros((T, T), F32)
    for i, (r, mine, x, x2, toward, back) in enumerate(((ru, top, 0, 1, 2, 1), (rd, bottom, 7, 6, 1, 2))):
        spot = lambda a: jnp.broadcast_to(r[2 * T : 2 * T + 1, a * T : (a + 1) * T], (8, T))
        cols = columns(seven(spot(0), spot(1), jnp.zeros((8, T), F32)))
        for j in (back, 4, 6):
            theirs[j] = spread(cols, j, 0)
        e = [wide[x, j] for j in range(7)]
        e2 = [wide[x2, j] for j in range(7)]
        b = [theirs[j] for j in range(7)]
        for h in range(8):
            d[:, tile(h)] = off(r[0:T, tile(h)], e, toward, 0)
        for h in range(8):
            vh = [a[h : h + 1, :] for a in v]
            mid = d[:, tile(h)]
            low = d[:, tile(h - 1)] if h > 0 else zero
            high = d[:, tile(h + 1)] if h < 7 else zero
            beside = r[T : 2 * T, tile(h)] + off(mine[0:T, tile(h)], b, back, 0)
            both = low + high
            value = (e[0] + (vh[0] + STEP / SECOND)) * mid + e[toward] * beside + vh[1] * high + vh[2] * low
            value = value + shifted(vh[3] * mid + vh[4] * both, vh[5] * mid + vh[6] * both, 1)
            value = value + shifted(e[3] * mid + e[4] * beside, e[5] * mid + e[6] * beside, 0)
            old = lambda at: cb[h // 7, tile(at), :] if h in (0, 7) else o[tile(at), tile(h)]
            rb[i, tile(i), tile(h)] = old(x) + SECOND * value
            rb[i, tile(1 - i), tile(h)] = old(x2) + SECOND * off(mid, e2, toward, 0)
        saves.append(copy(rb.at[i], out.at[pl.ds(6 * T * i, 2 * T), :], sem.at[3 + i]))
        saves[-1].start()
    for m in saves:
        m.wait()


def halo(o, top, bottom, left, right, ru, rd, fl, fr, wide, cw):
    scratch = [pltpu.VMEM((2, N, T), F32), pltpu.VMEM((2, 2 * T, N), F32), pltpu.VMEM((T, N), F32), pltpu.VMEM((7, T, T), F32), DMA((5,))]
    return call(halo_body, [((N, N), HBM)], scratch, [VMEM] * 11, "halo", 5)(o, top, bottom, left, right, ru, rd, fl, fr, wide, cw)[0]


@functools.cache
def weight_route(n):
    def place(r, c):
        half = n // 2
        return (2 * (c // half) + r // half, (c % half) // 2, r % half, c % 2)

    def far(a, b):
        ring = lambda d, size: min(d % size, -d % size)
        return ring(a[0] - b[0], 4) + ring(a[1] - b[1], max(n // 4, 1)) + ring(a[2] - b[2], n // 2) + 0.5 * (a[3] != b[3])

    pairs = []
    for c in range(n):
        cost = [[far(place(r, c), place(c, f)) for f in range(n)] for r in range(n)]
        for limit in sorted({x for row in cost for x in row}):
            taken = {}

            def find(r, seen):
                for f in sorted(range(n), key=lambda f: cost[r][f]):
                    if cost[r][f] <= limit and f not in seen:
                        seen.add(f)
                        if f not in taken or find(taken[f], seen):
                            taken[f] = r
                            return True
                return False

            if all(find(r, set()) for r in range(n)):
                break
        pairs += [(c * n + f, r * n + c) for f, r in taken.items()]
    return sorted(pairs)


def per_device(cov, noise, k, u, w):
    n_row, n_col = lax.axis_size("row"), lax.axis_size("col")

    def onward(a, axis, n):
        return lax.ppermute(a, axis, [(i, i + 1) for i in range(n - 1)])

    def back(a, axis, n):
        return lax.ppermute(a, axis, [(i + 1, i) for i in range(n - 1)])

    cov, noise, k, u, w = (pltpu.with_memory_space_constraint(a, pltpu.HBM) for a in (cov, noise, k, u, w))
    left, right, kuw = pack(cov, k, u, w)
    cw = lax.ppermute(kuw, ("row", "col"), weight_route(n_row))
    yl = onward(right, "col", n_col)
    yr = back(left, "col", n_col)
    top, bottom, wide = row_edges(cov, noise, kuw)
    top, bottom = row_finish(top, bottom, yl, yr, cw)
    ru = onward(bottom, "row", n_row)
    rd = back(top, "row", n_row)
    wide, top, bottom = lax.optimization_barrier((wide, top, bottom))
    left_f, right_f = col_edges(cov, noise, wide, cw)
    fl = onward(right_f, "col", n_col)
    fr = back(left_f, "col", n_col)
    o = block(cov, noise, yl, yr, wide, cw)
    return halo(o, top, bottom, left, right, ru, rd, fl, fr, wide, cw)


def solution(mesh):
    return jax.shard_map(
        per_device,
        mesh=mesh,
        in_specs=(P("row", "col"), P("row", "col"), P("row", None), P("row", None), P("row", None)),
        out_specs=P("row", "col"),
        check_vma=False,
    )
```

time: 211 us -> 68.8 us (0.33)
  other arithmetic: 104 us -> 0 us
  blocking collectives: 30 us -> 0 us
  local copies, waits for them, and re-layouts: 29.2 us -> 0 us
  Pallas kernels: 0 us -> 27.5 us
  starting transfers between devices: 35 us -> 22.7 us
  waiting for transfers between devices: 12 us -> 17.9 us
    add x6 -> x0, other arithmetic: 81.3 us -> none  [the longest x2 38.8 us: col_term(): total = total + weights[index][None, :, :] * piece]
    all_gather x1 -> x0, blocking collectives: 30 us -> none  [sent_together(): lax.all_gather(both, axis, axis=dim, tiled=True)]
    pallas_call x0 -> x6, Pallas kernels: none -> 27.5 us  [the longest x1 14.3 us: block(): call(block_body, [((N, N), VMEM)], scratch, [HBM, HBM] + [VMEM] * 4, 'blo...]
    concatenate x6 -> x0, other arithmetic: 22.5 us -> none  [the longest x5 22.5 us: extended(): jnp.concatenate([jnp.pad(low, around), value, jnp.pad(high, around)], axi...]
    slice x6 -> x0, local copies, waits for them, and re-layouts: 16.5 us -> none  [the longest x2 11.9 us: derive(): padded[side:side + rows, :].reshape(rows, cols // side + 2, side)]
    ppermute x8 -> x7, starting transfers between devices: 35 us -> 22.7 us  [the longest x3 12.5 us: onward(): return lax.ppermute(a, axis, [(i, i + 1) for i in range(n - 1)])]
    reshape x2 -> x0, local copies, waits for them, and re-layouts: 10.8 us -> none  [derive(): along_cols = col_term(middle_rows, col_weights).reshape(rows, cols)]
    ppermute x8 -> x7, waiting for transfers between devices: 12 us -> 17.9 us  [the longest x3 9.51 us: onward(): return lax.ppermute(a, axis, [(i, i + 1) for i in range(n - 1)])]
  transfers between devices with their start and end apart: 8 -> 7, of which waited for: 2 -> 4; matrix products, arithmetic and copies ran while one was open for 7% -> 0% of each run, Pallas kernels for 0% -> 29%
where the time goes in v2:
time: 68.8 us; the launch traced here: 68.4 us
  Pallas kernels  27.5 us (40%)
  starting transfers between devices  22.7 us (33%)
  waiting for transfers between devices  17.9 us (26%)
    pallas_call x1, Pallas kernels, block(): call(block_body, [((N, N), VMEM)], scratch, [HBM, HBM] + [VMEM] * 4, 'blo...  14.3 us
    ppermute x3, starting transfers between devices, onward(): return lax.ppermute(a, axis, [(i, i + 1) for i in range(n - 1)])  12.5 us
    ppermute x3, waiting for transfers between devices, onward(): return lax.ppermute(a, axis, [(i, i + 1) for i in range(n - 1)])  9.51 us
    pallas_call x1, Pallas kernels, halo(): call(halo_body, [((N, N), HBM)], scratch, [VMEM] * 11, 'halo', 5)  5.78 us
    ppermute x3, starting transfers between devices, back(): return lax.ppermute(a, axis, [(i + 1, i) for i in range(n - 1)])  5.31 us
    ppermute x1, starting transfers between devices, per_device(): cw = lax.ppermute(kuw, ('row', 'col'), weight_route(n_row))  4.86 us
    ppermute x3, waiting for transfers between devices, back(): return lax.ppermute(a, axis, [(i + 1, i) for i in range(n - 1)])  4.72 us
    ppermute x1, waiting for transfers between devices, per_device(): cw = lax.ppermute(kuw, ('row', 'col'), weight_route(n_row))  3.71 us
  transfers between devices with their start and end apart: 7, of which 4 were waited for; matrix products, arithmetic and copies ran while one was open for 0% of the time, Pallas kernels for 29%

profile of v2, /device:TPU:25, one launch (start us, length us, event | category | flops | bytes accessed | tf_op | source)
XLA Modules:
  0.0 68.4 jit_solution(16159069269209667714)
XLA Ops:
  0.0 1.3 %pack.1 = (f32[1024,128]{1,0:T(8,128)S(1)}, f32[1024,128]{1,0:T(8,128)S(1)}, f32[24,128]{1,0:T(8,128)S(1)}) custom-call(f32[1024,1024]{1,0:T(8,128)} %p.5, f32[8,128]{1,0:T(8,128)} %k.1, f32[8,128]{1,0:T(8,128)} %u.1, f32[8,128]{1,0:T(8,128)} %w.1), custom_call_target="tpu_custom_call" | custom-call | flops 1000000000 | bytes 3000000 | tf_op jit(solution)/shard_map/pack/pallas_call | solution.py:133
  1.3 4.9 %collective-permute-start = (f32[1024,128]{1,0:T(8,128)S(1)}, f32[1024,128]{1,0:T(8,128)S(1)}, u32[]{:S(2)}, u32[]{:S(2)}) collective-permute-start(f32[1024,128]{1,0:T(8,128)S(1)} %get-tuple-element.18.right), channel_id=1, source_target_pairs={{0,1},{1,2},{2,3},{3,4},{4,5},{5,6},{6,7},{7,8},{8,9},{9,10},{10,1... | collective-permute-start | bytes 1572872 | tf_op jit(solution)/shard_map/ppermute | solution.py:376
  6.2 1.9 %collective-permute-start.1 = (f32[1024,128]{1,0:T(8,128)S(1)}, f32[1024,128]{1,0:T(8,128)S(1)}, u32[]{:S(2)}, u32[]{:S(2)}) collective-permute-start(f32[1024,128]{1,0:T(8,128)S(1)} %get-tuple-element.19.left), channel_id=1, source_target_pairs={{1,0},{2,1},{3,2},{4,3},{5,4},{6,5},{7,6},{8,7},{9,8},{10,9},{11,1... | collective-permute-start | bytes 1572872 | tf_op jit(solution)/shard_map/ppermute | solution.py:379
  8.1 4.9 %collective-permute-start.2 = (f32[24,128]{1,0:T(8,128)S(1)}, f32[24,128]{1,0:T(8,128)S(1)}, u32[]{:S(2)}, u32[]{:S(2)}) collective-permute-start(f32[24,128]{1,0:T(8,128)S(1)} %get-tuple-element.20.kuw), channel_id=1, source_target_pairs={{0,240},{1,224},{2,176},{3,96},{4,48},{5,32},{6,64},{7,80},{8,192}... | collective-permute-start | bytes 36872 | tf_op jit(solution)/shard_map/ppermute | solution.py:383
  13.0 2.2 %row_edges.1 = (f32[264,1024]{1,0:T(8,128)S(1)}, f32[264,1024]{1,0:T(8,128)S(1)}, f32[8,7,128,128]{3,2,1,0:T(8,128)S(1)}) custom-call(f32[1024,1024]{1,0:T(8,128)} %p.5, f32[1024,1024]{1,0:T(8,128)} %q.3, f32[24,128]{1,0:T(8,128)S(1)} %get-tuple-element.20.kuw), custom_call_target="tpu_custom_call" | custom-call | flops 2000000000 | bytes 6000000 | tf_op jit(solution)/shard_map/row_edges/pallas_call | solution.py:167
  15.2 3.7 %collective-permute-done.2.cw = f32[24,128]{1,0:T(8,128)S(1)} collective-permute-done((f32[24,128]{1,0:T(8,128)S(1)}, f32[24,128]{1,0:T(8,128)S(1)}, u32[]{:S(2)}, u32[]{:S(2)}) %collective-permute-start.2) | collective-permute-done | bytes 12320 | tf_op jit(solution)/shard_map/ppermute | solution.py:383
  18.9 0.0 collective-permute-done.yl
  18.9 1.6 %collective-permute-done.1.yr = f32[1024,128]{1,0:T(8,128)S(1)} collective-permute-done((f32[1024,128]{1,0:T(8,128)S(1)}, f32[1024,128]{1,0:T(8,128)S(1)}, u32[]{:S(2)}, u32[]{:S(2)}) %collective-permute-start.1) | collective-permute-done | bytes 524320 | tf_op jit(solution)/shard_map/ppermute | solution.py:379
  20.6 0.7 %row_finish.1 = (f32[264,1024]{1,0:T(8,128)S(1)}, f32[264,1024]{1,0:T(8,128)S(1)}) custom-call(f32[264,1024]{1,0:T(8,128)S(1)} %get-tuple-element.22.top, f32[264,1024]{1,0:T(8,128)S(1)} %get-tuple-element.23.bottom, f32[1024,128]{1,0:T(8,128)S(1)} %collective-permute-done.yl, f32[1024,128]{1,0:T(8,128)S(1)} %collective-permute-done.1.yr, ...), custom_call_target="tpu_custom_call" | custom-call | flops 2000000000 | bytes 6000000 | tf_op jit(solution)/shard_map/row_finish/pallas_call | solution.py:185
  21.3 1.3 %collective-permute-start.4 = (f32[264,1024]{1,0:T(8,128)S(1)}, f32[264,1024]{1,0:T(8,128)S(1)}, u32[]{:S(2)}, u32[]{:S(2)}) collective-permute-start(f32[264,1024]{1,0:T(8,128)S(1)} %get-tuple-element.27.top), channel_id=1, source_target_pairs={{16,0},{32,16},{48,32},{64,48},{80,64},{96,80},{112,96},{128,112},... | collective-permute-start | bytes 3244040 | tf_op jit(solution)/shard_map/ppermute | solution.py:379
  22.6 4.1 %collective-permute-start.3 = (f32[264,1024]{1,0:T(8,128)S(1)}, f32[264,1024]{1,0:T(8,128)S(1)}, u32[]{:S(2)}, u32[]{:S(2)}) collective-permute-start(f32[264,1024]{1,0:T(8,128)S(1)} %get-tuple-element.28.bottom), channel_id=1, source_target_pairs={{0,16},{16,32},{32,48},{48,64},{64,80},{80,96},{96,112},{112,128},... | collective-permute-start | bytes 3244040 | tf_op jit(solution)/shard_map/ppermute | solution.py:376
  26.7 3.2 %col_edges.1 = (f32[1032,128]{1,0:T(8,128)S(1)}, f32[1032,128]{1,0:T(8,128)S(1)}) custom-call(f32[1024,1024]{1,0:T(8,128)} %p.5, f32[1024,1024]{1,0:T(8,128)} %q.3, f32[8,7,128,128]{3,2,1,0:T(8,128)S(1)} %get-tuple-element.26.wide, f32[24,128]{1,0:T(8,128)S(1)} %collective-permute-done.2.cw), custom_call_target="tpu_custom_call" | custom-call | flops 3000000000 | bytes 9000000 | tf_op jit(solution)/shard_map/col_edges/pallas_call | solution.py:217
  29.9 3.5 %collective-permute-start.5 = (f32[1032,128]{1,0:T(8,128)S(1)}, f32[1032,128]{1,0:T(8,128)S(1)}, u32[]{:S(2)}, u32[]{:S(2)}) collective-permute-start(f32[1032,128]{1,0:T(8,128)S(1)} %get-tuple-element.29), channel_id=1, source_target_pairs={{0,1},{1,2},{2,3},{3,4},{4,5},{5,6},{6,7},{7,8},{8,9},{9,10},{10,1... | collective-permute-start | bytes 1585160 | tf_op jit(solution)/shard_map/ppermute | solution.py:376
  33.4 2.1 %collective-permute-start.6 = (f32[1032,128]{1,0:T(8,128)S(1)}, f32[1032,128]{1,0:T(8,128)S(1)}, u32[]{:S(2)}, u32[]{:S(2)}) collective-permute-start(f32[1032,128]{1,0:T(8,128)S(1)} %get-tuple-element.30), channel_id=1, source_target_pairs={{1,0},{2,1},{3,2},{4,3},{5,4},{6,5},{7,6},{8,7},{9,8},{10,9},{11,1... | collective-permute-start | bytes 1585160 | tf_op jit(solution)/shard_map/ppermute | solution.py:379
  35.6 14.3 %block.1.o = f32[1024,1024]{1,0:T(8,128)S(1)} custom-call(f32[1024,1024]{1,0:T(8,128)} %p.5, f32[1024,1024]{1,0:T(8,128)} %q.3, f32[1024,128]{1,0:T(8,128)S(1)} %collective-permute-done.yl, f32[1024,128]{1,0:T(8,128)S(1)} %collective-permute-done.1.yr, f32[8,7,128,128]{3,2,1,0:T(8,128)S(1)} %get-tuple-element.26.wide, f32[24,128]{1,0:T(8,128)S(1)} %collective-permute-done.2.cw), custom_call_target="tpu_custom_call" | custom-call | flops 16000000000 | bytes 48000000 | tf_op jit(solution)/shard_map/block/pallas_call | solution.py:288
  49.9 9.5 %collective-permute-done.5.fl = f32[1032,128]{1,0:T(8,128)S(1)} collective-permute-done((f32[1032,128]{1,0:T(8,128)S(1)}, f32[1032,128]{1,0:T(8,128)S(1)}, u32[]{:S(2)}, u32[]{:S(2)}) %collective-permute-start.5) | collective-permute-done | bytes 528416 | tf_op jit(solution)/shard_map/ppermute | solution.py:376
  59.4 3.1 %collective-permute-done.6.fr = f32[1032,128]{1,0:T(8,128)S(1)} collective-permute-done((f32[1032,128]{1,0:T(8,128)S(1)}, f32[1032,128]{1,0:T(8,128)S(1)}, u32[]{:S(2)}, u32[]{:S(2)}) %collective-permute-start.6) | collective-permute-done | bytes 528416 | tf_op jit(solution)/shard_map/ppermute | solution.py:379
  62.5 0.0 collective-permute-done.4.rd
  62.5 0.0 collective-permute-done.3.ru
  62.5 5.8 %halo.1 = f32[1024,1024]{1,0:T(8,128)} custom-call(f32[1024,1024]{1,0:T(8,128)S(1)} %block.1.o, f32[264,1024]{1,0:T(8,128)S(1)} %get-tuple-element.27.top, f32[264,1024]{1,0:T(8,128)S(1)} %get-tuple-element.28.bottom, f32[1024,128]{1,0:T(8,128)S(1)} %get-tuple-element.19.left, f32[1024,128]{1,0:T(8,128)S(1)} %get-tuple-element.18.right, ...), custom_call_target="tpu_custom_call" | custom-call | flops 5000000000 | bytes 15000000 | tf_op jit(solution)/shard_map/halo/pallas_call | solution.py:338
Async XLA Ops:
  1.3 17.6 %collective-permute-start = (f32[1024,128]{1,0:T(8,128)S(1)}, f32[1024,128]{1,0:T(8,128)S(1)}, u32[]{:S(2)}, u32[]{:S(2)}) collective-permute-start(f32[1024,128]{1,0:T(8,128)S(1)} %get-tuple-element.18.right), channel_id=1, source_target_pairs={{0,1},{1,2},{2,3},{3,4},{4,5},{5,6},{6,7},{7,8},{8,9},{9,10},{10,1... | collective-permute-start | bytes 1572872 | tf_op jit(solution)/shard_map/ppermute | solution.py:376
  6.2 14.4 %collective-permute-start.1 = (f32[1024,128]{1,0:T(8,128)S(1)}, f32[1024,128]{1,0:T(8,128)S(1)}, u32[]{:S(2)}, u32[]{:S(2)}) collective-permute-start(f32[1024,128]{1,0:T(8,128)S(1)} %get-tuple-element.19.left), channel_id=1, source_target_pairs={{1,0},{2,1},{3,2},{4,3},{5,4},{6,5},{7,6},{8,7},{9,8},{10,9},{11,1... | collective-permute-start | bytes 1572872 | tf_op jit(solution)/shard_map/ppermute | solution.py:379
  8.1 10.8 %collective-permute-start.2 = (f32[24,128]{1,0:T(8,128)S(1)}, f32[24,128]{1,0:T(8,128)S(1)}, u32[]{:S(2)}, u32[]{:S(2)}) collective-permute-start(f32[24,128]{1,0:T(8,128)S(1)} %get-tuple-element.20.kuw), channel_id=1, source_target_pairs={{0,240},{1,224},{2,176},{3,96},{4,48},{5,32},{6,64},{7,80},{8,192}... | collective-permute-start | bytes 36872 | tf_op jit(solution)/shard_map/ppermute | solution.py:383
  21.3 41.2 %collective-permute-start.4 = (f32[264,1024]{1,0:T(8,128)S(1)}, f32[264,1024]{1,0:T(8,128)S(1)}, u32[]{:S(2)}, u32[]{:S(2)}) collective-permute-start(f32[264,1024]{1,0:T(8,128)S(1)} %get-tuple-element.27.top), channel_id=1, source_target_pairs={{16,0},{32,16},{48,32},{64,48},{80,64},{96,80},{112,96},{128,112},... | collective-permute-start | bytes 3244040 | tf_op jit(solution)/shard_map/ppermute | solution.py:379
  22.6 39.9 %collective-permute-start.3 = (f32[264,1024]{1,0:T(8,128)S(1)}, f32[264,1024]{1,0:T(8,128)S(1)}, u32[]{:S(2)}, u32[]{:S(2)}) collective-permute-start(f32[264,1024]{1,0:T(8,128)S(1)} %get-tuple-element.28.bottom), channel_id=1, source_target_pairs={{0,16},{16,32},{32,48},{48,64},{64,80},{80,96},{96,112},{112,128},... | collective-permute-start | bytes 3244040 | tf_op jit(solution)/shard_map/ppermute | solution.py:376
  29.9 29.5 %collective-permute-start.5 = (f32[1032,128]{1,0:T(8,128)S(1)}, f32[1032,128]{1,0:T(8,128)S(1)}, u32[]{:S(2)}, u32[]{:S(2)}) collective-permute-start(f32[1032,128]{1,0:T(8,128)S(1)} %get-tuple-element.29), channel_id=1, source_target_pairs={{0,1},{1,2},{2,3},{3,4},{4,5},{5,6},{6,7},{7,8},{8,9},{9,10},{10,1... | collective-permute-start | bytes 1585160 | tf_op jit(solution)/shard_map/ppermute | solution.py:376
  33.4 29.0 %collective-permute-start.6 = (f32[1032,128]{1,0:T(8,128)S(1)}, f32[1032,128]{1,0:T(8,128)S(1)}, u32[]{:S(2)}, u32[]{:S(2)}) collective-permute-start(f32[1032,128]{1,0:T(8,128)S(1)} %get-tuple-element.30), channel_id=1, source_target_pairs={{1,0},{2,1},{3,2},{4,3},{5,4},{6,5},{7,6},{8,7},{9,8},{10,9},{11,1... | collective-permute-start | bytes 1585160 | tf_op jit(solution)/shard_map/ppermute | solution.py:379

commit v3 on v2

--- a/solution.py
+++ b/solution.py
@@ -56,6 +56,18 @@
 def full(mid, low, high, w, axis):
     both = low + high
     return w[0] * mid + w[1] * high + w[2] * low + shifted(w[3] * mid + w[4] * both, w[5] * mid + w[6] * both, axis)
+
+
+def stencil(mid, above, below, left, right, e, v):
+    value = (e[0] + v[0]) * mid
+    for low, high, w, axis in ((left, right, v, 1), (above, below, e, 0)):
+        both = low if high is None else high if low is None else low + high
+        if high is not None:
+            value = value + w[1] * high
+        if low is not None:
+            value = value + w[2] * low
+        value = value + shifted(w[3] * mid + w[4] * both, w[5] * mid + w[6] * both, axis)
+    return value
 
 
 def off(value, w, side, axis):
@@ -98,7 +110,7 @@
     return pl.ds(pl.multiple_of(i * T, T), T)
 
 
-def call(body, out, scratch, ins, name, us):
+def call(body, out, scratch, ins, name, us, aliases=None):
     shapes = [jax.ShapeDtypeStruct(s, F32) for s, _ in out]
     specs = [space for _, space in out]
     return pl.pallas_call(
@@ -107,7 +119,8 @@
         out_specs=specs,
         out_shape=shapes,
         scratch_shapes=scratch,
-        compiler_params=pltpu.CompilerParams(vmem_limit_bytes=40 << 20),
+        input_output_aliases=aliases or {},
+        compiler_params=pltpu.CompilerParams(vmem_limit_bytes=14 << 20),
         cost_estimate=pl.CostEstimate(flops=us * 10**9, transcendentals=0, bytes_accessed=us * 3 * 10**6),
         name=name,
     )
@@ -171,8 +184,6 @@
     v = seven(*tables(cw))
     for i, (src, out) in enumerate(((top, top_out), (bottom, bottom_out))):
         rows = pl.ds(7 * T * i, T)
-        out[0:T, :] = src[0:T, :]
-        out[2 * T : 2 * T + 8, :] = src[2 * T : 2 * T + 8, :]
         for h in range(8):
             low = 2.0 * yl[rows, :] if h == 0 else src[0:T, tile(h - 1)]
             high = 2.0 * yr[rows, :] if h == 7 else src[0:T, tile(h + 1)]
@@ -182,16 +193,10 @@
 
 def row_finish(top, bottom, yl, yr, cw):
     edge = ((2 * T + 8, N), VMEM)
-    return call(row_finish_body, [edge, edge], [], [VMEM] * 5, "row_finish", 2)(top, bottom, yl, yr, cw)
-
-
-def col_edges_body(p, q, wide, cw, left, right, pb, qb, sem):
-    moves = []
-    for s in range(2):
-        moves.append(copy(p.at[:, pl.ds(6 * T * s, 2 * T)], pb.at[s], sem.at[2 * s]))
-        moves.append(copy(q.at[:, pl.ds(7 * T * s, T)], qb.at[s], sem.at[2 * s + 1]))
-    for m in moves:
-        m.start()
+    return call(row_finish_body, [edge, edge], [], [VMEM] * 5, "row_finish", 1, {0: 0, 1: 1})(top, bottom, yl, yr, cw)
+
+
+def col_edges_body(p, q, wide, cw, left, right):
     kuw = tables(cw)
     zero = jnp.zeros((T, T), F32)
     for s, h, out in ((0, 0, left), (1, 7, right)):
@@ -200,111 +205,47 @@
             out[N + i : N + i + 1, :] = kuw[i][h : h + 1, :]
         near, far = right_factor(kuw, h, "own"), right_factor(kuw, h, "before" if s else "next")
         factor = split(jnp.concatenate([far, near] if s else [near, far], axis=0))
-        moves[2 * s].wait()
-        moves[2 * s + 1].wait()
-        mine = tile(s)
-        out[0:N, :] = times(pb[s], factor)
+        out[0:N, :] = times(p[:, 6 * T * s : 6 * T * s + 2 * T], factor)
         for x in range(8):
             e = [wide[x, j] for j in range(7)]
-            low = zero if x == 0 else pb[s, tile(x - 1), mine]
-            high = zero if x == 7 else pb[s, tile(x + 1), mine]
-            out[tile(x), :] = out[tile(x), :] + (qb[s, tile(x), :] + full(pb[s, tile(x), mine], low, high, e, 0))
+            low = zero if x == 0 else p[tile(x - 1), tile(h)]
+            high = zero if x == 7 else p[tile(x + 1), tile(h)]
+            out[tile(x), :] = out[tile(x), :] + (q[tile(x), tile(h)] + full(p[tile(x), tile(h)], low, high, e, 0))
 
 
 def col_edges(cov, noise, wide, cw):
     edge = ((N + 8, T), VMEM)
-    scratch = [pltpu.VMEM((2, N, 2 * T), F32), pltpu.VMEM((2, N, T), F32), DMA((4,))]
-    return call(col_edges_body, [edge, edge], scratch, [HBM, HBM] + [VMEM] * 2, "col_edges", 3)(cov, noise, wide, cw)
-
-
-def block_body(p_hbm, q_hbm, yl, yr, wide, cw, o, pe, fe, v_s, sem_p, sem_q):
-    def load_p(x):
-        return copy(p_hbm.at[tile(x), :], pe.at[pl.ds((x + 1) * T, T), pl.ds(T, N)], sem_p.at[x])
-
-    def load_q(x):
-        return copy(q_hbm.at[tile(x), :], o.at[tile(x), :], sem_q.at[x])
-
-    for x in range(8):
-        load_p(x).start()
-        load_q(x).start()
-    inner = slice(T, 9 * T)
-    pe[inner, 0:T] = yl[...]
-    pe[inner, 9 * T : 10 * T] = yr[...]
-    fe[inner, 0:T] = jnp.zeros((N, T), F32)
-    fe[inner, 9 * T : 10 * T] = jnp.zeros((N, T), F32)
-    for r in (pe, fe):
-        r[0:T, inner] = jnp.zeros((T, N), F32)
-        r[9 * T : 10 * T, inner] = jnp.zeros((T, N), F32)
+    return call(col_edges_body, [edge, edge], [], [VMEM] * 4, "col_edges", 2)(cov, noise, wide, cw)
+
+
+def block_body(p, q, yl, yr, wide, cw, o, f):
     v = seven(*tables(cw))
-    for x in range(8):
-        for j in range(7):
-            v_s[0, x, j] = jnp.broadcast_to(v[j][x : x + 1, :], (8, T))
-        v_s[1, x, 0] = jnp.broadcast_to(v[0][x : x + 1, :] + STEP / SECOND, (8, T))
-        for j in range(1, 7):
-            v_s[1, x, j] = v_s[0, x, j]
-
-    def apply(src, x, h, stage):
+    vs = [[a[h : h + 1, :] for a in v] for h in range(8)]
+    vs2 = [[w[0] + STEP / SECOND] + w[1:] for w in vs]
+
+    def apply(src, left, right, x, h, w):
+        row = lambda i: src[tile(i), tile(h)] if 0 <= i < 8 else None
+        col = lambda i: src[tile(x), tile(i)] if 0 <= i < 8 else (left if i < 0 else right)
         e = [wide[x, j] for j in range(7)]
-        v = [v_s[stage, h, j, 0:1, :] for j in range(7)]
-        rows = pl.ds((x + 1) * T, T)
-        mid, low, high = (src[rows, at_tile(h + i)] for i in (1, 0, 2))
-        both = low + high
-        value = (e[0] + v[0]) * mid + v[1] * high + v[2] * low
-        value = value + shifted(v[3] * mid + v[4] * both, v[5] * mid + v[6] * both, 1)
-        low, high = (src[pl.ds((x + i) * T, T), at_tile(h + 1)] for i in (0, 2))
-        both = low + high
-        value = value + e[1] * high + e[2] * low
-        return value + shifted(e[3] * mid + e[4] * both, e[5] * mid + e[6] * both, 0)
-
-    def first(x):
-        @pl.loop(0, 8, unroll=8)
-        def _(h):
-            fe[pl.ds((x + 1) * T, T), at_tile(h + 1)] = o[tile(x), at_tile(h)] + apply(pe, x, h, 0)
-
-    def second(x):
-        @pl.loop(0, 8, unroll=8)
-        def _(h):
-            o[tile(x), at_tile(h)] = pe[pl.ds((x + 1) * T, T), at_tile(h + 1)] + SECOND * apply(fe, x, h, 1)
-
-    load_p(0).wait()
+        return stencil(row(x), row(x - 1), row(x + 1), col(h - 1), col(h + 1), e, w[h])
+
     for x in range(9):
         if x < 8:
-            if x < 7:
-                load_p(x + 1).wait()
-            load_q(x).wait()
-            first(x)
+            for h in range(8):
+                f[tile(x), tile(h)] = q[tile(x), tile(h)] + apply(p, yl[tile(x), :], yr[tile(x), :], x, h, vs)
         if x > 0:
-            second(x - 1)
+            for h in range(8):
+                o[tile(x - 1), tile(h)] = p[tile(x - 1), tile(h)] + SECOND * apply(f, None, None, x - 1, h, vs2)
 
 
 def block(cov, noise, yl, yr, wide, cw):
-    scratch = [
-        pltpu.VMEM((10 * T, 10 * T), F32),
-        pltpu.VMEM((10 * T, 10 * T), F32),
-        pltpu.VMEM((2, 8, 7, 8, T), F32),
-        DMA((8,)),
-        DMA((8,)),
-    ]
-    return call(block_body, [((N, N), VMEM)], scratch, [HBM, HBM] + [VMEM] * 4, "block", 16)(cov, noise, yl, yr, wide, cw)[0]
-
-
-def halo_body(o, top, bottom, left, right, ru, rd, fl, fr, wide, cw, out, cb, rb, d, theirs, sem):
-    inner = copy(o.at[pl.ds(2 * T, 4 * T), pl.ds(T, 6 * T)], out.at[pl.ds(2 * T, 4 * T), pl.ds(T, 6 * T)], sem.at[0])
-    inner.start()
-    saves = [inner]
+    return call(block_body, [((N, N), VMEM)], [pltpu.VMEM((N, N), F32)], [VMEM] * 6, "block", 12)(cov, noise, yl, yr, wide, cw)[0]
+
+
+def row_halo_body(o_in, top, bottom, ru, rd, wide, cw, o, d, theirs):
     v = seven(*tables(cw))
-    for s, (f, mine, h, toward, back) in enumerate(((fl, left, 0, 2, 1), (fr, right, 7, 1, 2))):
-        spot = lambda i: jnp.broadcast_to(f[N + i : N + i + 1, :], (8, T))
-        b = [a[0:1, :] for a in seven(spot(0), spot(1), jnp.zeros((8, T), F32))]
-        vh = [a[h : h + 1, :] for a in v]
-        for x in range(8):
-            beside = f[tile(x), :] + off(mine[tile(x), :], b, back, 1)
-            cb[s, tile(x), :] = o[tile(x), tile(h)] + SECOND * off(beside, vh, toward, 1)
-        rows = pl.ds(2 * T, 4 * T)
-        saves.append(copy(cb.at[s, rows, :], out.at[rows, pl.ds(7 * T * s, T)], sem.at[1 + s]))
-        saves[-1].start()
-    zero = jnp.zeros((T, T), F32)
-    for i, (r, mine, x, x2, toward, back) in enumerate(((ru, top, 0, 1, 2, 1), (rd, bottom, 7, 6, 1, 2))):
+    get = lambda ref, h: ref[0:T, tile(h)] if 0 <= h < 8 else jnp.zeros((T, T), F32)
+    for r, mine, x, x2, toward, back in ((ru, top, 0, 1, 2, 1), (rd, bottom, 7, 6, 1, 2)):
         spot = lambda a: jnp.broadcast_to(r[2 * T : 2 * T + 1, a * T : (a + 1) * T], (8, T))
         cols = columns(seven(spot(0), spot(1), jnp.zeros((8, T), F32)))
         for j in (back, 4, 6):
@@ -317,25 +258,42 @@
         for h in range(8):
             vh = [a[h : h + 1, :] for a in v]
             mid = d[:, tile(h)]
-            low = d[:, tile(h - 1)] if h > 0 else zero
-            high = d[:, tile(h + 1)] if h < 7 else zero
             beside = r[T : 2 * T, tile(h)] + off(mine[0:T, tile(h)], b, back, 0)
+            low, high = get(d, h - 1), get(d, h + 1)
             both = low + high
             value = (e[0] + (vh[0] + STEP / SECOND)) * mid + e[toward] * beside + vh[1] * high + vh[2] * low
             value = value + shifted(vh[3] * mid + vh[4] * both, vh[5] * mid + vh[6] * both, 1)
             value = value + shifted(e[3] * mid + e[4] * beside, e[5] * mid + e[6] * beside, 0)
-            old = lambda at: cb[h // 7, tile(at), :] if h in (0, 7) else o[tile(at), tile(h)]
-            rb[i, tile(i), tile(h)] = old(x) + SECOND * value
-            rb[i, tile(1 - i), tile(h)] = old(x2) + SECOND * off(mid, e2, toward, 0)
-        saves.append(copy(rb.at[i], out.at[pl.ds(6 * T * i, 2 * T), :], sem.at[3 + i]))
+            o[tile(x), tile(h)] = o_in[tile(x), tile(h)] + SECOND * value
+            o[tile(x2), tile(h)] = o_in[tile(x2), tile(h)] + SECOND * off(mid, e2, toward, 0)
+
+
+def row_halo(*args):
+    scratch = [pltpu.VMEM((T, N), F32), pltpu.VMEM((7, T, T), F32)]
+    return call(row_halo_body, [((N, N), VMEM)], scratch, [VMEM] * 7, "row_halo", 4, {0: 0})(*args)[0]
+
+
+def col_halo_body(o, left, right, fl, fr, cw, out, cb, sem):
+    inner = copy(o.at[:, pl.ds(T, 6 * T)], out.at[:, pl.ds(T, 6 * T)], sem.at[0])
+    inner.start()
+    saves = [inner]
+    v = seven(*tables(cw))
+    for s, (f, mine, h, toward, back) in enumerate(((fl, left, 0, 2, 1), (fr, right, 7, 1, 2))):
+        spot = lambda i: jnp.broadcast_to(f[N + i : N + i + 1, :], (8, T))
+        b = [a[0:1, :] for a in seven(spot(0), spot(1), jnp.zeros((8, T), F32))]
+        vh = [a[h : h + 1, :] for a in v]
+        for x in range(8):
+            beside = f[tile(x), :] + off(mine[tile(x), :], b, back, 1)
+            cb[s, tile(x), :] = o[tile(x), tile(h)] + SECOND * off(beside, vh, toward, 1)
+        saves.append(copy(cb.at[s], out.at[:, pl.ds(7 * T * s, T)], sem.at[1 + s]))
         saves[-1].start()
     for m in saves:
         m.wait()
 
 
-def halo(o, top, bottom, left, right, ru, rd, fl, fr, wide, cw):
-    scratch = [pltpu.VMEM((2, N, T), F32), pltpu.VMEM((2, 2 * T, N), F32), pltpu.VMEM((T, N), F32), pltpu.VMEM((7, T, T), F32), DMA((5,))]
-    return call(halo_body, [((N, N), HBM)], scratch, [VMEM] * 11, "halo", 5)(o, top, bottom, left, right, ru, rd, fl, fr, wide, cw)[0]
+def col_halo(*args):
+    scratch = [pltpu.VMEM((2, N, T), F32), DMA((3,))]
+    return call(col_halo_body, [((N, N), HBM)], scratch, [VMEM] * 6, "col_halo", 2)(*args)[0]
 
 
 @functools.cache
@@ -378,12 +336,13 @@
     def back(a, axis, n):
         return lax.ppermute(a, axis, [(i + 1, i) for i in range(n - 1)])
 
-    cov, noise, k, u, w = (pltpu.with_memory_space_constraint(a, pltpu.HBM) for a in (cov, noise, k, u, w))
-    left, right, kuw = pack(cov, k, u, w)
+    in_hbm = lambda a: pltpu.with_memory_space_constraint(a, pltpu.HBM)
+    cov_hbm, noise_hbm = in_hbm(cov), in_hbm(noise)
+    left, right, kuw = pack(cov_hbm, in_hbm(k), in_hbm(u), in_hbm(w))
     cw = lax.ppermute(kuw, ("row", "col"), weight_route(n_row))
     yl = onward(right, "col", n_col)
     yr = back(left, "col", n_col)
-    top, bottom, wide = row_edges(cov, noise, kuw)
+    top, bottom, wide = row_edges(cov_hbm, noise_hbm, kuw)
     top, bottom = row_finish(top, bottom, yl, yr, cw)
     ru = onward(bottom, "row", n_row)
     rd = back(top, "row", n_row)
@@ -392,7 +351,8 @@
     fl = onward(right_f, "col", n_col)
     fr = back(left_f, "col", n_col)
     o = block(cov, noise, yl, yr, wide, cw)
-    return halo(o, top, bottom, left, right, ru, rd, fl, fr, wide, cw)
+    o = row_halo(o, top, bottom, ru, rd, wide, cw)
+    return col_halo(o, left, right, fl, fr, cw)
 
 
 def solution(mesh):

time: 68.8 us -> 63.6 us (0.924)
  Pallas kernels: 27.5 us -> 22.8 us
    ppermute x3, waiting for transfers between devices: 9.51 us -> 4.6 us  [onward(): return lax.ppermute(a, axis, [(i, i + 1) for i in range(n - 1)])]
    pallas_call x4 -> x5, Pallas kernels: 24 us -> 19.2 us  [the longest x1 10.7 us: block(): call(block_body, [((N, N), VMEM)], [pltpu.VMEM((N, N), F32)], [VMEM] * 6,...]
    ppermute x3, waiting for transfers between devices: 4.72 us -> 9.43 us  [back(): return lax.ppermute(a, axis, [(i + 1, i) for i in range(n - 1)])]
  transfers between devices with their start and end apart: 7 -> 7, of which waited for: 4 -> 6; matrix products, arithmetic and copies ran while one was open for 0% -> 0% of each run, Pallas kernels for 29% -> 28%
where the time goes in v3:
time: 63.6 us; the launch traced here: 62.8 us
  Pallas kernels  22.8 us (36%)
  starting transfers between devices  22.1 us (35%)
  waiting for transfers between devices  17.6 us (28%)
    ppermute x3, starting transfers between devices, onward(): return lax.ppermute(a, axis, [(i, i + 1) for i in range(n - 1)])  11.9 us
    pallas_call x1, Pallas kernels, block(): call(block_body, [((N, N), VMEM)], [pltpu.VMEM((N, N), F32)], [VMEM] * 6,...  10.7 us
    ppermute x3, waiting for transfers between devices, back(): return lax.ppermute(a, axis, [(i + 1, i) for i in range(n - 1)])  9.43 us
    ppermute x3, starting transfers between devices, back(): return lax.ppermute(a, axis, [(i + 1, i) for i in range(n - 1)])  5.31 us
    ppermute x1, starting transfers between devices, per_device(): cw = lax.ppermute(kuw, ('row', 'col'), weight_route(n_row))  4.86 us
    ppermute x3, waiting for transfers between devices, onward(): return lax.ppermute(a, axis, [(i, i + 1) for i in range(n - 1)])  4.6 us
    ppermute x1, waiting for transfers between devices, per_device(): cw = lax.ppermute(kuw, ('row', 'col'), weight_route(n_row))  3.56 us
    pallas_call x1, Pallas kernels, row_halo(): call(row_halo_body, [((N, N), VMEM)], scratch, [VMEM] * 7, 'row_halo', 4,...  2.89 us
  transfers between devices with their start and end apart: 7, of which 6 were waited for; matrix products, arithmetic and copies ran while one was open for 0% of the time, Pallas kernels for 28%

profile of v3, /device:TPU:25, one launch (start us, length us, event | category | flops | bytes accessed | tf_op | source)
XLA Modules:
  0.0 62.8 jit_solution(12108342114366818662)
XLA Ops:
  0.0 1.3 %pack.1 = (f32[1024,128]{1,0:T(8,128)S(1)}, f32[1024,128]{1,0:T(8,128)S(1)}, f32[24,128]{1,0:T(8,128)S(1)}) custom-call(f32[1024,1024]{1,0:T(8,128)} %p.7, f32[8,128]{1,0:T(8,128)} %k.1, f32[8,128]{1,0:T(8,128)} %u.1, f32[8,128]{1,0:T(8,128)} %w.1), custom_call_target="tpu_custom_call" | custom-call | flops 1000000000 | bytes 3000000 | tf_op jit(solution)/shard_map/pack/pallas_call | solution.py:146
  1.3 4.9 %collective-permute-start = (f32[1024,128]{1,0:T(8,128)S(1)}, f32[1024,128]{1,0:T(8,128)S(1)}, u32[]{:S(2)}, u32[]{:S(2)}) collective-permute-start(f32[1024,128]{1,0:T(8,128)S(1)} %get-tuple-element.18.right), channel_id=1, source_target_pairs={{0,1},{1,2},{2,3},{3,4},{4,5},{5,6},{6,7},{7,8},{8,9},{9,10},{10,1... | collective-permute-start | bytes 1572872 | tf_op jit(solution)/shard_map/ppermute | solution.py:334
  6.2 1.9 %collective-permute-start.1 = (f32[1024,128]{1,0:T(8,128)S(1)}, f32[1024,128]{1,0:T(8,128)S(1)}, u32[]{:S(2)}, u32[]{:S(2)}) collective-permute-start(f32[1024,128]{1,0:T(8,128)S(1)} %get-tuple-element.19.left), channel_id=1, source_target_pairs={{1,0},{2,1},{3,2},{4,3},{5,4},{6,5},{7,6},{8,7},{9,8},{10,9},{11,1... | collective-permute-start | bytes 1572872 | tf_op jit(solution)/shard_map/ppermute | solution.py:337
  8.1 4.9 %collective-permute-start.2 = (f32[24,128]{1,0:T(8,128)S(1)}, f32[24,128]{1,0:T(8,128)S(1)}, u32[]{:S(2)}, u32[]{:S(2)}) collective-permute-start(f32[24,128]{1,0:T(8,128)S(1)} %get-tuple-element.20.kuw), channel_id=1, source_target_pairs={{0,240},{1,224},{2,176},{3,96},{4,48},{5,32},{6,64},{7,80},{8,192}... | collective-permute-start | bytes 36872 | tf_op jit(solution)/shard_map/ppermute | solution.py:342
  13.0 0.0 copy-start
  13.0 0.0 copy-start.1
  13.0 2.3 %row_edges.1 = (f32[264,1024]{1,0:T(8,128)S(1)}, f32[264,1024]{1,0:T(8,128)S(1)}, f32[8,7,128,128]{3,2,1,0:T(8,128)S(1)}) custom-call(f32[1024,1024]{1,0:T(8,128)} %p.7, f32[1024,1024]{1,0:T(8,128)} %q.5, f32[24,128]{1,0:T(8,128)S(1)} %get-tuple-element.20.kuw), custom_call_target="tpu_custom_call" | custom-call | flops 2000000000 | bytes 6000000 | tf_op jit(solution)/shard_map/row_edges/pallas_call | solution.py:180
  15.4 3.6 %collective-permute-done.2.cw = f32[24,128]{1,0:T(8,128)S(1)} collective-permute-done((f32[24,128]{1,0:T(8,128)S(1)}, f32[24,128]{1,0:T(8,128)S(1)}, u32[]{:S(2)}, u32[]{:S(2)}) %collective-permute-start.2) | collective-permute-done | bytes 12320 | tf_op jit(solution)/shard_map/ppermute | solution.py:342
  18.9 0.0 collective-permute-done.yl
  18.9 1.6 %collective-permute-done.1.yr = f32[1024,128]{1,0:T(8,128)S(1)} collective-permute-done((f32[1024,128]{1,0:T(8,128)S(1)}, f32[1024,128]{1,0:T(8,128)S(1)}, u32[]{:S(2)}, u32[]{:S(2)}) %collective-permute-start.1) | collective-permute-done | bytes 524320 | tf_op jit(solution)/shard_map/ppermute | solution.py:337
  20.6 1.2 %row_finish.1 = (f32[264,1024]{1,0:T(8,128)S(1)}, f32[264,1024]{1,0:T(8,128)S(1)}) custom-call(f32[264,1024]{1,0:T(8,128)S(1)} %get-tuple-element.22.top, f32[264,1024]{1,0:T(8,128)S(1)} %get-tuple-element.23.bottom, f32[1024,128]{1,0:T(8,128)S(1)} %collective-permute-done.yl, ...), custom_call_target="tpu_custom_call", output_to_operand_aliasing={{0}: (0, {}), {1}: (1, {})} | custom-call | flops 1000000000 | bytes 3000000 | tf_op jit(solution)/shard_map/row_finish/pallas_call | solution.py:196
  21.8 3.5 %collective-permute-start.3 = (f32[264,1024]{1,0:T(8,128)S(1)}, f32[264,1024]{1,0:T(8,128)S(1)}, u32[]{:S(2)}, u32[]{:S(2)}) collective-permute-start(f32[264,1024]{1,0:T(8,128)S(1)} %get-tuple-element.28.bottom), channel_id=1, source_target_pairs={{0,16},{16,32},{32,48},{48,64},{64,80},{80,96},{96,112},{112,128},... | collective-permute-start | bytes 3244040 | tf_op jit(solution)/shard_map/ppermute | solution.py:334
  25.3 1.3 %collective-permute-start.4 = (f32[264,1024]{1,0:T(8,128)S(1)}, f32[264,1024]{1,0:T(8,128)S(1)}, u32[]{:S(2)}, u32[]{:S(2)}) collective-permute-start(f32[264,1024]{1,0:T(8,128)S(1)} %get-tuple-element.27.top), channel_id=1, source_target_pairs={{16,0},{32,16},{48,32},{64,48},{80,64},{96,80},{112,96},{128,112},... | collective-permute-start | bytes 3244040 | tf_op jit(solution)/shard_map/ppermute | solution.py:337
  26.6 0.0 copy-done
  26.6 0.0 copy-done.1
  26.6 1.5 %col_edges.1 = (f32[1032,128]{1,0:T(8,128)S(1)}, f32[1032,128]{1,0:T(8,128)S(1)}) custom-call(f32[1024,1024]{1,0:T(8,128)S(1)} %copy-done, f32[1024,1024]{1,0:T(8,128)S(1)} %copy-done.1, f32[8,7,128,128]{3,2,1,0:T(8,128)S(1)} %get-tuple-element.26.wide, f32[24,128]{1,0:T(8,128)S(1)} %collective-permute-done.2.cw), custom_call_target="tpu_custom_call" | custom-call | flops 2000000000 | bytes 6000000 | tf_op jit(solution)/shard_map/col_edges/pallas_call | solution.py:218
  28.1 3.5 %collective-permute-start.5 = (f32[1032,128]{1,0:T(8,128)S(1)}, f32[1032,128]{1,0:T(8,128)S(1)}, u32[]{:S(2)}, u32[]{:S(2)}) collective-permute-start(f32[1032,128]{1,0:T(8,128)S(1)} %get-tuple-element.29), channel_id=1, source_target_pairs={{0,1},{1,2},{2,3},{3,4},{4,5},{5,6},{6,7},{7,8},{8,9},{9,10},{10,1... | collective-permute-start | bytes 1585160 | tf_op jit(solution)/shard_map/ppermute | solution.py:334
  31.7 2.1 %collective-permute-start.6 = (f32[1032,128]{1,0:T(8,128)S(1)}, f32[1032,128]{1,0:T(8,128)S(1)}, u32[]{:S(2)}, u32[]{:S(2)}) collective-permute-start(f32[1032,128]{1,0:T(8,128)S(1)} %get-tuple-element.30), channel_id=1, source_target_pairs={{1,0},{2,1},{3,2},{4,3},{5,4},{6,5},{7,6},{8,7},{9,8},{10,9},{11,1... | collective-permute-start | bytes 1585160 | tf_op jit(solution)/shard_map/ppermute | solution.py:337
  33.8 10.7 %block.1.o_in = f32[1024,1024]{1,0:T(8,128)S(1)} custom-call(f32[1024,1024]{1,0:T(8,128)S(1)} %copy-done, f32[1024,1024]{1,0:T(8,128)S(1)} %copy-done.1, f32[1024,128]{1,0:T(8,128)S(1)} %collective-permute-done.yl, f32[1024,128]{1,0:T(8,128)S(1)} %collective-permute-done.1.yr, f32[8,7,128,128]{3,2,1,0:T(8,128)S(1)} %get-tuple-element.26.wide, ...), custom_call_target="tpu_custom_call" | custom-call | flops 12000000000 | bytes 36000000 | tf_op jit(solution)/shard_map/block/pallas_call | solution.py:242
  44.4 1.4 %collective-permute-done.3.ru = f32[264,1024]{1,0:T(8,128)S(1)} collective-permute-done((f32[264,1024]{1,0:T(8,128)S(1)}, f32[264,1024]{1,0:T(8,128)S(1)}, u32[]{:S(2)}, u32[]{:S(2)}) %collective-permute-start.3) | collective-permute-done | bytes 1081376 | tf_op jit(solution)/shard_map/ppermute | solution.py:334
  45.9 5.0 %collective-permute-done.4.rd = f32[264,1024]{1,0:T(8,128)S(1)} collective-permute-done((f32[264,1024]{1,0:T(8,128)S(1)}, f32[264,1024]{1,0:T(8,128)S(1)}, u32[]{:S(2)}, u32[]{:S(2)}) %collective-permute-start.4) | collective-permute-done | bytes 1081376 | tf_op jit(solution)/shard_map/ppermute | solution.py:337
  50.9 2.9 %row_halo.1.o = f32[1024,1024]{1,0:T(8,128)S(1)} custom-call(f32[1024,1024]{1,0:T(8,128)S(1)} %block.1.o_in, f32[264,1024]{1,0:T(8,128)S(1)} %get-tuple-element.27.top, f32[264,1024]{1,0:T(8,128)S(1)} %get-tuple-element.28.bottom, f32[264,1024]{1,0:T(8,128)S(1)} %collective-permute-done.3.ru, ...), custom_call_target="tpu_custom_call", output_to_operand_aliasing={{}: (0, {})} | custom-call | flops 4000000000 | bytes 12000000 | tf_op jit(solution)/shard_map/row_halo/pallas_call | solution.py:273
  53.8 3.2 %collective-permute-done.5.fl = f32[1032,128]{1,0:T(8,128)S(1)} collective-permute-done((f32[1032,128]{1,0:T(8,128)S(1)}, f32[1032,128]{1,0:T(8,128)S(1)}, u32[]{:S(2)}, u32[]{:S(2)}) %collective-permute-start.5) | collective-permute-done | bytes 528416 | tf_op jit(solution)/shard_map/ppermute | solution.py:334
  57.0 2.8 %collective-permute-done.6.fr = f32[1032,128]{1,0:T(8,128)S(1)} collective-permute-done((f32[1032,128]{1,0:T(8,128)S(1)}, f32[1032,128]{1,0:T(8,128)S(1)}, u32[]{:S(2)}, u32[]{:S(2)}) %collective-permute-start.6) | collective-permute-done | bytes 528416 | tf_op jit(solution)/shard_map/ppermute | solution.py:337
  59.7 2.9 %col_halo.1 = f32[1024,1024]{1,0:T(8,128)} custom-call(f32[1024,1024]{1,0:T(8,128)S(1)} %row_halo.1.o, f32[1024,128]{1,0:T(8,128)S(1)} %get-tuple-element.19.left, f32[1024,128]{1,0:T(8,128)S(1)} %get-tuple-element.18.right, f32[1032,128]{1,0:T(8,128)S(1)} %collective-permute-done.5.fl, f32[1032,128]{1,0:T(8,128)S(1)} %collective-permute-done.6.fr, ...), custom_call_target="tpu_custom_call" | custom-call | flops 2000000000 | bytes 6000000 | tf_op jit(solution)/shard_map/col_halo/pallas_call | solution.py:296
Async XLA Ops:
  1.3 17.6 %collective-permute-start = (f32[1024,128]{1,0:T(8,128)S(1)}, f32[1024,128]{1,0:T(8,128)S(1)}, u32[]{:S(2)}, u32[]{:S(2)}) collective-permute-start(f32[1024,128]{1,0:T(8,128)S(1)} %get-tuple-element.18.right), channel_id=1, source_target_pairs={{0,1},{1,2},{2,3},{3,4},{4,5},{5,6},{6,7},{7,8},{8,9},{9,10},{10,1... | collective-permute-start | bytes 1572872 | tf_op jit(solution)/shard_map/ppermute | solution.py:334
  6.2 14.4 %collective-permute-start.1 = (f32[1024,128]{1,0:T(8,128)S(1)}, f32[1024,128]{1,0:T(8,128)S(1)}, u32[]{:S(2)}, u32[]{:S(2)}) collective-permute-start(f32[1024,128]{1,0:T(8,128)S(1)} %get-tuple-element.19.left), channel_id=1, source_target_pairs={{1,0},{2,1},{3,2},{4,3},{5,4},{6,5},{7,6},{8,7},{9,8},{10,9},{11,1... | collective-permute-start | bytes 1572872 | tf_op jit(solution)/shard_map/ppermute | solution.py:337
  8.1 10.8 %collective-permute-start.2 = (f32[24,128]{1,0:T(8,128)S(1)}, f32[24,128]{1,0:T(8,128)S(1)}, u32[]{:S(2)}, u32[]{:S(2)}) collective-permute-start(f32[24,128]{1,0:T(8,128)S(1)} %get-tuple-element.20.kuw), channel_id=1, source_target_pairs={{0,240},{1,224},{2,176},{3,96},{4,48},{5,32},{6,64},{7,80},{8,192}... | collective-permute-start | bytes 36872 | tf_op jit(solution)/shard_map/ppermute | solution.py:342
  13.0 13.6 %copy-start = (f32[1024,1024]{1,0:T(8,128)S(1)}, f32[1024,1024]{1,0:T(8,128)}, u32[]{:S(2)}) copy-start(f32[1024,1024]{1,0:T(8,128)} %p.7) | copy-start | bytes 12582916
  13.0 13.6 %copy-start.1 = (f32[1024,1024]{1,0:T(8,128)S(1)}, f32[1024,1024]{1,0:T(8,128)}, u32[]{:S(2)}) copy-start(f32[1024,1024]{1,0:T(8,128)} %q.5) | copy-start | bytes 12582916
  21.8 24.1 %collective-permute-start.3 = (f32[264,1024]{1,0:T(8,128)S(1)}, f32[264,1024]{1,0:T(8,128)S(1)}, u32[]{:S(2)}, u32[]{:S(2)}) collective-permute-start(f32[264,1024]{1,0:T(8,128)S(1)} %get-tuple-element.28.bottom), channel_id=1, source_target_pairs={{0,16},{16,32},{32,48},{48,64},{64,80},{80,96},{96,112},{112,128},... | collective-permute-start | bytes 3244040 | tf_op jit(solution)/shard_map/ppermute | solution.py:334
  25.3 25.6 %collective-permute-start.4 = (f32[264,1024]{1,0:T(8,128)S(1)}, f32[264,1024]{1,0:T(8,128)S(1)}, u32[]{:S(2)}, u32[]{:S(2)}) collective-permute-start(f32[264,1024]{1,0:T(8,128)S(1)} %get-tuple-element.27.top), channel_id=1, source_target_pairs={{16,0},{32,16},{48,32},{64,48},{80,64},{96,80},{112,96},{128,112},... | collective-permute-start | bytes 3244040 | tf_op jit(solution)/shard_map/ppermute | solution.py:337
  28.1 28.9 %collective-permute-start.5 = (f32[1032,128]{1,0:T(8,128)S(1)}, f32[1032,128]{1,0:T(8,128)S(1)}, u32[]{:S(2)}, u32[]{:S(2)}) collective-permute-start(f32[1032,128]{1,0:T(8,128)S(1)} %get-tuple-element.29), channel_id=1, source_target_pairs={{0,1},{1,2},{2,3},{3,4},{4,5},{5,6},{6,7},{7,8},{8,9},{9,10},{10,1... | collective-permute-start | bytes 1585160 | tf_op jit(solution)/shard_map/ppermute | solution.py:334
  31.7 28.1 %collective-permute-start.6 = (f32[1032,128]{1,0:T(8,128)S(1)}, f32[1032,128]{1,0:T(8,128)S(1)}, u32[]{:S(2)}, u32[]{:S(2)}) collective-permute-start(f32[1032,128]{1,0:T(8,128)S(1)} %get-tuple-element.30), channel_id=1, source_target_pairs={{1,0},{2,1},{3,2},{4,3},{5,4},{6,5},{7,6},{8,7},{9,8},{10,9},{11,1... | collective-permute-start | bytes 1585160 | tf_op jit(solution)/shard_map/ppermute | solution.py:337

commit v4 on v3

--- a/solution.py
+++ b/solution.py
@@ -184,6 +184,8 @@
     v = seven(*tables(cw))
     for i, (src, out) in enumerate(((top, top_out), (bottom, bottom_out))):
         rows = pl.ds(7 * T * i, T)
+        out[0:T, :] = src[0:T, :]
+        out[2 * T : 2 * T + 8, :] = src[2 * T : 2 * T + 8, :]
         for h in range(8):
             low = 2.0 * yl[rows, :] if h == 0 else src[0:T, tile(h - 1)]
             high = 2.0 * yr[rows, :] if h == 7 else src[0:T, tile(h + 1)]
@@ -193,7 +195,7 @@
 
 def row_finish(top, bottom, yl, yr, cw):
     edge = ((2 * T + 8, N), VMEM)
-    return call(row_finish_body, [edge, edge], [], [VMEM] * 5, "row_finish", 1, {0: 0, 1: 1})(top, bottom, yl, yr, cw)
+    return call(row_finish_body, [edge, edge], [], [VMEM] * 5, "row_finish", 1)(top, bottom, yl, yr, cw)
 
 
 def col_edges_body(p, q, wide, cw, left, right):
@@ -285,14 +287,16 @@
         for x in range(8):
             beside = f[tile(x), :] + off(mine[tile(x), :], b, back, 1)
             cb[s, tile(x), :] = o[tile(x), tile(h)] + SECOND * off(beside, vh, toward, 1)
-        saves.append(copy(cb.at[s], out.at[:, pl.ds(7 * T * s, T)], sem.at[1 + s]))
-        saves[-1].start()
+            if x % 4 == 3:
+                rows = pl.ds((x - 3) * T, 4 * T)
+                saves.append(copy(cb.at[s, rows, :], out.at[rows, pl.ds(7 * T * s, T)], sem.at[len(saves)]))
+                saves[-1].start()
     for m in saves:
         m.wait()
 
 
 def col_halo(*args):
-    scratch = [pltpu.VMEM((2, N, T), F32), DMA((3,))]
+    scratch = [pltpu.VMEM((2, N, T), F32), DMA((5,))]
     return call(col_halo_body, [((N, N), HBM)], scratch, [VMEM] * 6, "col_halo", 2)(*args)[0]
 
 

time: 63.6 us -> 63.2 us (level)
  no operation moved by 1% of the time
where the time goes in v4:
time: 63.2 us; the launch traced here: 62.4 us
  Pallas kernels  22.3 us (35%)
  starting transfers between devices  22.1 us (35%)
  waiting for transfers between devices  17.7 us (28%)
    ppermute x3, starting transfers between devices, onward(): return lax.ppermute(a, axis, [(i, i + 1) for i in range(n - 1)])  11.9 us
    pallas_call x1, Pallas kernels, block(): call(block_body, [((N, N), VMEM)], [pltpu.VMEM((N, N), F32)], [VMEM] * 6,...  10.7 us
    ppermute x3, waiting for transfers between devices, back(): return lax.ppermute(a, axis, [(i + 1, i) for i in range(n - 1)])  9.29 us
    ppermute x3, starting transfers between devices, back(): return lax.ppermute(a, axis, [(i + 1, i) for i in range(n - 1)])  5.31 us
    ppermute x1, starting transfers between devices, per_device(): cw = lax.ppermute(kuw, ('row', 'col'), weight_route(n_row))  4.86 us
    ppermute x3, waiting for transfers between devices, onward(): return lax.ppermute(a, axis, [(i, i + 1) for i in range(n - 1)])  4.83 us
    ppermute x1, waiting for transfers between devices, per_device(): cw = lax.ppermute(kuw, ('row', 'col'), weight_route(n_row))  3.55 us
    pallas_call x1, Pallas kernels, row_halo(): call(row_halo_body, [((N, N), VMEM)], scratch, [VMEM] * 7, 'row_halo', 4,...  2.96 us
  transfers between devices with their start and end apart: 7, of which 6 were waited for; matrix products, arithmetic and copies ran while one was open for 0% of the time, Pallas kernels for 28%

profile of v4, /device:TPU:25, one launch (start us, length us, event | category | flops | bytes accessed | tf_op | source)
XLA Modules:
  0.0 62.4 jit_solution(16355014639284276552)
XLA Ops:
  0.0 1.3 %pack.1 = (f32[1024,128]{1,0:T(8,128)S(1)}, f32[1024,128]{1,0:T(8,128)S(1)}, f32[24,128]{1,0:T(8,128)S(1)}) custom-call(f32[1024,1024]{1,0:T(8,128)} %p.7, f32[8,128]{1,0:T(8,128)} %k.1, f32[8,128]{1,0:T(8,128)} %u.1, f32[8,128]{1,0:T(8,128)} %w.1), custom_call_target="tpu_custom_call" | custom-call | flops 1000000000 | bytes 3000000 | tf_op jit(solution)/shard_map/pack/pallas_call | solution.py:146
  1.3 4.9 %collective-permute-start = (f32[1024,128]{1,0:T(8,128)S(1)}, f32[1024,128]{1,0:T(8,128)S(1)}, u32[]{:S(2)}, u32[]{:S(2)}) collective-permute-start(f32[1024,128]{1,0:T(8,128)S(1)} %get-tuple-element.18.right), channel_id=1, source_target_pairs={{0,1},{1,2},{2,3},{3,4},{4,5},{5,6},{6,7},{7,8},{8,9},{9,10},{10,1... | collective-permute-start | bytes 1572872 | tf_op jit(solution)/shard_map/ppermute | solution.py:338
  6.2 1.9 %collective-permute-start.1 = (f32[1024,128]{1,0:T(8,128)S(1)}, f32[1024,128]{1,0:T(8,128)S(1)}, u32[]{:S(2)}, u32[]{:S(2)}) collective-permute-start(f32[1024,128]{1,0:T(8,128)S(1)} %get-tuple-element.19.left), channel_id=1, source_target_pairs={{1,0},{2,1},{3,2},{4,3},{5,4},{6,5},{7,6},{8,7},{9,8},{10,9},{11,1... | collective-permute-start | bytes 1572872 | tf_op jit(solution)/shard_map/ppermute | solution.py:341
  8.1 4.9 %collective-permute-start.2 = (f32[24,128]{1,0:T(8,128)S(1)}, f32[24,128]{1,0:T(8,128)S(1)}, u32[]{:S(2)}, u32[]{:S(2)}) collective-permute-start(f32[24,128]{1,0:T(8,128)S(1)} %get-tuple-element.20.kuw), channel_id=1, source_target_pairs={{0,240},{1,224},{2,176},{3,96},{4,48},{5,32},{6,64},{7,80},{8,192}... | collective-permute-start | bytes 36872 | tf_op jit(solution)/shard_map/ppermute | solution.py:346
  13.0 0.0 copy-start
  13.0 0.0 copy-start.1
  13.0 2.4 %row_edges.1 = (f32[264,1024]{1,0:T(8,128)S(1)}, f32[264,1024]{1,0:T(8,128)S(1)}, f32[8,7,128,128]{3,2,1,0:T(8,128)S(1)}) custom-call(f32[1024,1024]{1,0:T(8,128)} %p.7, f32[1024,1024]{1,0:T(8,128)} %q.5, f32[24,128]{1,0:T(8,128)S(1)} %get-tuple-element.20.kuw), custom_call_target="tpu_custom_call" | custom-call | flops 2000000000 | bytes 6000000 | tf_op jit(solution)/shard_map/row_edges/pallas_call | solution.py:180
  15.4 3.5 %collective-permute-done.2.cw = f32[24,128]{1,0:T(8,128)S(1)} collective-permute-done((f32[24,128]{1,0:T(8,128)S(1)}, f32[24,128]{1,0:T(8,128)S(1)}, u32[]{:S(2)}, u32[]{:S(2)}) %collective-permute-start.2) | collective-permute-done | bytes 12320 | tf_op jit(solution)/shard_map/ppermute | solution.py:346
  18.9 0.0 collective-permute-done.yl
  18.9 1.6 %collective-permute-done.1.yr = f32[1024,128]{1,0:T(8,128)S(1)} collective-permute-done((f32[1024,128]{1,0:T(8,128)S(1)}, f32[1024,128]{1,0:T(8,128)S(1)}, u32[]{:S(2)}, u32[]{:S(2)}) %collective-permute-start.1) | collective-permute-done | bytes 524320 | tf_op jit(solution)/shard_map/ppermute | solution.py:341
  20.6 0.7 %row_finish.1 = (f32[264,1024]{1,0:T(8,128)S(1)}, f32[264,1024]{1,0:T(8,128)S(1)}) custom-call(f32[264,1024]{1,0:T(8,128)S(1)} %get-tuple-element.22.top, f32[264,1024]{1,0:T(8,128)S(1)} %get-tuple-element.23.bottom, f32[1024,128]{1,0:T(8,128)S(1)} %collective-permute-done.yl, f32[1024,128]{1,0:T(8,128)S(1)} %collective-permute-done.1.yr, ...), custom_call_target="tpu_custom_call" | custom-call | flops 1000000000 | bytes 3000000 | tf_op jit(solution)/shard_map/row_finish/pallas_call | solution.py:198
  21.3 3.5 %collective-permute-start.3 = (f32[264,1024]{1,0:T(8,128)S(1)}, f32[264,1024]{1,0:T(8,128)S(1)}, u32[]{:S(2)}, u32[]{:S(2)}) collective-permute-start(f32[264,1024]{1,0:T(8,128)S(1)} %get-tuple-element.28.bottom), channel_id=1, source_target_pairs={{0,16},{16,32},{32,48},{48,64},{64,80},{80,96},{96,112},{112,128},... | collective-permute-start | bytes 3244040 | tf_op jit(solution)/shard_map/ppermute | solution.py:338
  24.8 1.3 %collective-permute-start.4 = (f32[264,1024]{1,0:T(8,128)S(1)}, f32[264,1024]{1,0:T(8,128)S(1)}, u32[]{:S(2)}, u32[]{:S(2)}) collective-permute-start(f32[264,1024]{1,0:T(8,128)S(1)} %get-tuple-element.27.top), channel_id=1, source_target_pairs={{16,0},{32,16},{48,32},{64,48},{80,64},{96,80},{112,96},{128,112},... | collective-permute-start | bytes 3244040 | tf_op jit(solution)/shard_map/ppermute | solution.py:341
  26.1 0.0 copy-done
  26.1 0.0 copy-done.1
  26.1 1.5 %col_edges.1 = (f32[1032,128]{1,0:T(8,128)S(1)}, f32[1032,128]{1,0:T(8,128)S(1)}) custom-call(f32[1024,1024]{1,0:T(8,128)S(1)} %copy-done, f32[1024,1024]{1,0:T(8,128)S(1)} %copy-done.1, f32[8,7,128,128]{3,2,1,0:T(8,128)S(1)} %get-tuple-element.26.wide, f32[24,128]{1,0:T(8,128)S(1)} %collective-permute-done.2.cw), custom_call_target="tpu_custom_call" | custom-call | flops 2000000000 | bytes 6000000 | tf_op jit(solution)/shard_map/col_edges/pallas_call | solution.py:220
  27.6 3.5 %collective-permute-start.5 = (f32[1032,128]{1,0:T(8,128)S(1)}, f32[1032,128]{1,0:T(8,128)S(1)}, u32[]{:S(2)}, u32[]{:S(2)}) collective-permute-start(f32[1032,128]{1,0:T(8,128)S(1)} %get-tuple-element.29), channel_id=1, source_target_pairs={{0,1},{1,2},{2,3},{3,4},{4,5},{5,6},{6,7},{7,8},{8,9},{9,10},{10,1... | collective-permute-start | bytes 1585160 | tf_op jit(solution)/shard_map/ppermute | solution.py:338
  31.2 2.1 %collective-permute-start.6 = (f32[1032,128]{1,0:T(8,128)S(1)}, f32[1032,128]{1,0:T(8,128)S(1)}, u32[]{:S(2)}, u32[]{:S(2)}) collective-permute-start(f32[1032,128]{1,0:T(8,128)S(1)} %get-tuple-element.30), channel_id=1, source_target_pairs={{1,0},{2,1},{3,2},{4,3},{5,4},{6,5},{7,6},{8,7},{9,8},{10,9},{11,1... | collective-permute-start | bytes 1585160 | tf_op jit(solution)/shard_map/ppermute | solution.py:341
  33.3 10.7 %block.1.o_in = f32[1024,1024]{1,0:T(8,128)S(1)} custom-call(f32[1024,1024]{1,0:T(8,128)S(1)} %copy-done, f32[1024,1024]{1,0:T(8,128)S(1)} %copy-done.1, f32[1024,128]{1,0:T(8,128)S(1)} %collective-permute-done.yl, f32[1024,128]{1,0:T(8,128)S(1)} %collective-permute-done.1.yr, f32[8,7,128,128]{3,2,1,0:T(8,128)S(1)} %get-tuple-element.26.wide, ...), custom_call_target="tpu_custom_call" | custom-call | flops 12000000000 | bytes 36000000 | tf_op jit(solution)/shard_map/block/pallas_call | solution.py:244
  44.0 1.6 %collective-permute-done.3.ru = f32[264,1024]{1,0:T(8,128)S(1)} collective-permute-done((f32[264,1024]{1,0:T(8,128)S(1)}, f32[264,1024]{1,0:T(8,128)S(1)}, u32[]{:S(2)}, u32[]{:S(2)}) %collective-permute-start.3) | collective-permute-done | bytes 1081376 | tf_op jit(solution)/shard_map/ppermute | solution.py:338
  45.5 4.9 %collective-permute-done.4.rd = f32[264,1024]{1,0:T(8,128)S(1)} collective-permute-done((f32[264,1024]{1,0:T(8,128)S(1)}, f32[264,1024]{1,0:T(8,128)S(1)}, u32[]{:S(2)}, u32[]{:S(2)}) %collective-permute-start.4) | collective-permute-done | bytes 1081376 | tf_op jit(solution)/shard_map/ppermute | solution.py:341
  50.4 3.0 %row_halo.1.o = f32[1024,1024]{1,0:T(8,128)S(1)} custom-call(f32[1024,1024]{1,0:T(8,128)S(1)} %block.1.o_in, f32[264,1024]{1,0:T(8,128)S(1)} %get-tuple-element.27.top, f32[264,1024]{1,0:T(8,128)S(1)} %get-tuple-element.28.bottom, f32[264,1024]{1,0:T(8,128)S(1)} %collective-permute-done.3.ru, ...), custom_call_target="tpu_custom_call", output_to_operand_aliasing={{}: (0, {})} | custom-call | flops 4000000000 | bytes 12000000 | tf_op jit(solution)/shard_map/row_halo/pallas_call | solution.py:275
  53.4 3.3 %collective-permute-done.5.fl = f32[1032,128]{1,0:T(8,128)S(1)} collective-permute-done((f32[1032,128]{1,0:T(8,128)S(1)}, f32[1032,128]{1,0:T(8,128)S(1)}, u32[]{:S(2)}, u32[]{:S(2)}) %collective-permute-start.5) | collective-permute-done | bytes 528416 | tf_op jit(solution)/shard_map/ppermute | solution.py:338
  56.6 2.8 %collective-permute-done.6.fr = f32[1032,128]{1,0:T(8,128)S(1)} collective-permute-done((f32[1032,128]{1,0:T(8,128)S(1)}, f32[1032,128]{1,0:T(8,128)S(1)}, u32[]{:S(2)}, u32[]{:S(2)}) %collective-permute-start.6) | collective-permute-done | bytes 528416 | tf_op jit(solution)/shard_map/ppermute | solution.py:341
  59.4 2.8 %col_halo.1 = f32[1024,1024]{1,0:T(8,128)} custom-call(f32[1024,1024]{1,0:T(8,128)S(1)} %row_halo.1.o, f32[1024,128]{1,0:T(8,128)S(1)} %get-tuple-element.19.left, f32[1024,128]{1,0:T(8,128)S(1)} %get-tuple-element.18.right, f32[1032,128]{1,0:T(8,128)S(1)} %collective-permute-done.5.fl, f32[1032,128]{1,0:T(8,128)S(1)} %collective-permute-done.6.fr, ...), custom_call_target="tpu_custom_call" | custom-call | flops 2000000000 | bytes 6000000 | tf_op jit(solution)/shard_map/col_halo/pallas_call | solution.py:300
Async XLA Ops:
  1.3 17.6 %collective-permute-start = (f32[1024,128]{1,0:T(8,128)S(1)}, f32[1024,128]{1,0:T(8,128)S(1)}, u32[]{:S(2)}, u32[]{:S(2)}) collective-permute-start(f32[1024,128]{1,0:T(8,128)S(1)} %get-tuple-element.18.right), channel_id=1, source_target_pairs={{0,1},{1,2},{2,3},{3,4},{4,5},{5,6},{6,7},{7,8},{8,9},{9,10},{10,1... | collective-permute-start | bytes 1572872 | tf_op jit(solution)/shard_map/ppermute | solution.py:338
  6.2 14.4 %collective-permute-start.1 = (f32[1024,128]{1,0:T(8,128)S(1)}, f32[1024,128]{1,0:T(8,128)S(1)}, u32[]{:S(2)}, u32[]{:S(2)}) collective-permute-start(f32[1024,128]{1,0:T(8,128)S(1)} %get-tuple-element.19.left), channel_id=1, source_target_pairs={{1,0},{2,1},{3,2},{4,3},{5,4},{6,5},{7,6},{8,7},{9,8},{10,9},{11,1... | collective-permute-start | bytes 1572872 | tf_op jit(solution)/shard_map/ppermute | solution.py:341
  8.1 10.8 %collective-permute-start.2 = (f32[24,128]{1,0:T(8,128)S(1)}, f32[24,128]{1,0:T(8,128)S(1)}, u32[]{:S(2)}, u32[]{:S(2)}) collective-permute-start(f32[24,128]{1,0:T(8,128)S(1)} %get-tuple-element.20.kuw), channel_id=1, source_target_pairs={{0,240},{1,224},{2,176},{3,96},{4,48},{5,32},{6,64},{7,80},{8,192}... | collective-permute-start | bytes 36872 | tf_op jit(solution)/shard_map/ppermute | solution.py:346
  13.0 13.1 %copy-start = (f32[1024,1024]{1,0:T(8,128)S(1)}, f32[1024,1024]{1,0:T(8,128)}, u32[]{:S(2)}) copy-start(f32[1024,1024]{1,0:T(8,128)} %p.7) | copy-start | bytes 12582916
  13.0 13.1 %copy-start.1 = (f32[1024,1024]{1,0:T(8,128)S(1)}, f32[1024,1024]{1,0:T(8,128)}, u32[]{:S(2)}) copy-start(f32[1024,1024]{1,0:T(8,128)} %q.5) | copy-start | bytes 12582916
  21.3 24.2 %collective-permute-start.3 = (f32[264,1024]{1,0:T(8,128)S(1)}, f32[264,1024]{1,0:T(8,128)S(1)}, u32[]{:S(2)}, u32[]{:S(2)}) collective-permute-start(f32[264,1024]{1,0:T(8,128)S(1)} %get-tuple-element.28.bottom), channel_id=1, source_target_pairs={{0,16},{16,32},{32,48},{48,64},{64,80},{80,96},{96,112},{112,128},... | collective-permute-start | bytes 3244040 | tf_op jit(solution)/shard_map/ppermute | solution.py:338
  24.8 25.6 %collective-permute-start.4 = (f32[264,1024]{1,0:T(8,128)S(1)}, f32[264,1024]{1,0:T(8,128)S(1)}, u32[]{:S(2)}, u32[]{:S(2)}) collective-permute-start(f32[264,1024]{1,0:T(8,128)S(1)} %get-tuple-element.27.top), channel_id=1, source_target_pairs={{16,0},{32,16},{48,32},{64,48},{80,64},{96,80},{112,96},{128,112},... | collective-permute-start | bytes 3244040 | tf_op jit(solution)/shard_map/ppermute | solution.py:341
  27.6 29.0 %collective-permute-start.5 = (f32[1032,128]{1,0:T(8,128)S(1)}, f32[1032,128]{1,0:T(8,128)S(1)}, u32[]{:S(2)}, u32[]{:S(2)}) collective-permute-start(f32[1032,128]{1,0:T(8,128)S(1)} %get-tuple-element.29), channel_id=1, source_target_pairs={{0,1},{1,2},{2,3},{3,4},{4,5},{5,6},{6,7},{7,8},{8,9},{9,10},{10,1... | collective-permute-start | bytes 1585160 | tf_op jit(solution)/shard_map/ppermute | solution.py:338
  31.2 28.2 %collective-permute-start.6 = (f32[1032,128]{1,0:T(8,128)S(1)}, f32[1032,128]{1,0:T(8,128)S(1)}, u32[]{:S(2)}, u32[]{:S(2)}) collective-permute-start(f32[1032,128]{1,0:T(8,128)S(1)} %get-tuple-element.30), channel_id=1, source_target_pairs={{1,0},{2,1},{3,2},{4,3},{5,4},{6,5},{7,6},{8,7},{9,8},{10,9},{11,1... | collective-permute-start | bytes 1585160 | tf_op jit(solution)/shard_map/ppermute | solution.py:341
